TPU v7x, 256 devices: a whole 4x4x8 slice. The times are simulated.
256 devices in a mesh: section: 8 (over z_lo, core), dp: 32 (over y, x, z_hi).
Axes of the slice: x: 4, y: 4, z: 8 (z_hi: 2, z_lo: 4; z = z_hi * 4 + z_lo), core: 2. Of those that a mesh axis runs over, the one named last changes fastest.
Arguments:
- clips: bfloat16 [8, 32, 4, 8, 8, 128], P(None, 'dp'), may hold values from -6 to 6
- cotangent: bfloat16 [8, 32, 4, 8, 8, 128], P(None, 'dp'), may hold values from -6 to 6
- weights: bfloat16 [8, 3456, 128], P('section', 'dp'), may hold values from -0.078125 to 0.078125
Outputs:
- section_outs: bfloat16 [8, 8, 32, 4, 8, 8, 128], P('section', None, 'dp')
- weight_grads: float32 [8, 3456, 128], P('section', 'dp')
All inputs are finite; a program needn't handle non-finite values.
Results may differ from a plain program's by a relative error of at most 0.027.
Values may be sent and summed in bfloat16 or wider, within the bound.
A program may use at most 64 MiB of HBM per device.

v0:
```python
import jax
import jax.numpy as jnp
from jax import lax
from jax.sharding import PartitionSpec as P


def passed_along(block, axis, distance):
    devices = range(lax.axis_size(axis))
    route = [(i - distance, i) for i in devices if i - distance in devices]
    return lax.ppermute(block, axis, route)


def gather_patches(field):
    frames, height, width, channels = field.shape
    first_frame = field[:1]
    padded = jnp.concatenate([first_frame, first_frame, field], axis=0)
    padded = jnp.pad(padded, ((0, 0), (1, 1), (1, 1), (0, 0)))
    pieces = [
        padded[
            offset_time : offset_time + frames,
            offset_row : offset_row + height,
            offset_col : offset_col + width,
        ]
        for offset_time in range(3)
        for offset_row in range(3)
        for offset_col in range(3)
    ]
    return jnp.stack(pieces, axis=3).reshape(frames * height * width, 27 * channels)


def squash_field(activation):
    return jax.nn.silu(activation.astype(jnp.float32)).astype(jnp.bfloat16)


def squash_columns(activation):
    return gather_patches(squash_field(activation))


def layer_forward(activation, weight):
    branch = jnp.dot(squash_columns(activation), weight, preferred_element_type=jnp.float32)
    return (activation.astype(jnp.float32) + branch.reshape(activation.shape)).astype(jnp.bfloat16)


def input_gradient(activation, upstream, weight):
    flat_grad = upstream.reshape(-1, weight.shape[1])
    column_grad = lax.dot_general(
        flat_grad, weight, (((1,), (1,)), ((), ())), preferred_element_type=jnp.float32
    )
    base = activation.astype(jnp.float32)
    _, unfold = jax.vjp(gather_patches, base)
    field_grad = unfold(column_grad)[0]
    sigmoid_value = jax.nn.sigmoid(base)
    slope = sigmoid_value * (1.0 + base * (1.0 - sigmoid_value))
    return (upstream.astype(jnp.float32) + field_grad * slope).astype(jnp.bfloat16)


def weight_term(activation, upstream):
    flat_grad = upstream.reshape(-1, upstream.shape[-1])
    return lax.dot_general(
        squash_columns(activation),
        flat_grad,
        (((0,), (0,)), ((), ())),
        preferred_element_type=jnp.float32,
    )


def per_device(clips, cotangent, weights):
    section_total = lax.axis_size("section")
    section_index = lax.axis_index("section")
    weight = lax.all_gather(weights, "dp", axis=1, tiled=True)[0]
    local_clips = clips[:, 0]
    local_grads = cotangent[:, 0]
    micro_count = local_clips.shape[0]
    step_count = micro_count + section_total - 1
    empty_field = jnp.zeros(local_clips.shape[1:], jnp.bfloat16)

    def forward_step(step_index, carry):
        received, saved_inputs, produced = carry
        micro_index = step_index - section_index
        active = (micro_index >= 0) & (micro_index < micro_count)
        slot_index = jnp.clip(micro_index, 0, micro_count - 1)
        fresh = lax.dynamic_index_in_dim(local_clips, slot_index, 0, keepdims=False)
        layer_input = jnp.where(section_index == 0, fresh, received)
        layer_output = layer_forward(layer_input, weight)
        kept_input = jnp.where(
            active,
            layer_input,
            lax.dynamic_index_in_dim(saved_inputs, slot_index, 0, keepdims=False),
        )
        kept_output = jnp.where(
            active, layer_output, lax.dynamic_index_in_dim(produced, slot_index, 0, keepdims=False)
        )
        saved_inputs = lax.dynamic_update_index_in_dim(saved_inputs, kept_input, slot_index, 0)
        produced = lax.dynamic_update_index_in_dim(produced, kept_output, slot_index, 0)
        received = passed_along(layer_output, "section", 1)
        return (received, saved_inputs, produced)

    start_forward = (empty_field, jnp.zeros_like(local_clips), jnp.zeros_like(local_clips))
    _, saved_inputs, produced = lax.fori_loop(0, step_count, forward_step, start_forward)

    def backward_step(step_index, carry):
        received, grad_total, kept_grads = carry
        micro_index = step_index - (section_total - 1 - section_index)
        active = (micro_index >= 0) & (micro_index < micro_count)
        slot_index = jnp.clip(micro_index, 0, micro_count - 1)
        fresh = lax.dynamic_index_in_dim(local_grads, slot_index, 0, keepdims=False)
        upstream = jnp.where(section_index == section_total - 1, fresh, received)
        activation = lax.dynamic_index_in_dim(saved_inputs, slot_index, 0, keepdims=False)
        grad_total = grad_total + jnp.where(active, weight_term(activation, upstream), 0.0)
        layer_grad = input_gradient(activation, upstream, weight)
        received = passed_along(layer_grad, "section", -1)
        return (received, grad_total, kept_grads)

    start_backward = (
        empty_field,
        jnp.zeros(weight.shape, jnp.float32),
        jnp.zeros_like(local_grads),
    )
    _, grad_total, kept_grads = lax.fori_loop(0, step_count, backward_step, start_backward)
    grad_share = lax.psum_scatter(
        grad_total.astype(jnp.bfloat16), "dp", scatter_dimension=0, tiled=True
    ).astype(jnp.float32)
    return (produced[None, :, None], grad_share[None])


def solution(mesh):
    placed = (
        P(None, "dp", None, None, None, None),
        P(None, "dp", None, None, None, None),
        P("section", "dp", None),
    )
    return jax.shard_map(
        per_device,
        mesh=mesh,
        in_specs=placed,
        out_specs=(P("section", None, "dp", None, None, None, None), P("section", "dp", None)),
        check_vma=False,
    )
```

profile of v0, /device:TPU:98, one launch (start us, length us, event | category | flops | bytes accessed | tf_op | source)
XLA Modules:
  0.0 626.4 jit_solution(11397557660246506297)
XLA Ops:
  1.4 153.5 %all_gather.3 = bf16[1,3456,128]{2,0,1:T(2,128)(2,1)S(1)} all-gather(bf16[1,108,128]{2,0,1:T(2,128)(2,1)S(1)} %copy.118), channel_id=1, replica_groups=mesh['section'=8,'dp'=32] {'dp'}, dimensions={1}, use_global_device_ids=true | all-gather | bytes 912384 | tf_op jit(solution)/shard_map/all_gather | solution.py:70
  157.0 159.6 %while.37 = (s32[]{:T(128)}, bf16[4,8,8,128]{3,2,1,0:T(8,128)(2,1)S(1)}, bf16[8,4,8,8,128]{4,3,2,1,0:T(8,128)(2,1)}, bf16[8,4,8,8,128]{4,3,2,1,0:T(8,128)(2,1)S(...) while((s32[]{:T(128)}, ...), condition=%wide.region_1.2_spmd, body=%wide.region_0.1_spmd.sunk | while | flops 227311616 | bytes 8454884 | solution.py:99
  162.1 1.9 collective-permute-start
  164.0 3.7 collective-permute-done
  172.8 1.9 collective-permute-start
  174.7 3.7 collective-permute-done
  183.4 1.9 collective-permute-start
  185.3 3.7 collective-permute-done
  194.0 1.9 collective-permute-start
  196.0 3.7 collective-permute-done
  204.7 1.9 collective-permute-start
  206.6 3.7 collective-permute-done
  215.3 1.9 collective-permute-start
  217.3 3.7 collective-permute-done
  226.0 1.9 collective-permute-start
  227.9 3.7 collective-permute-done
  236.6 1.9 collective-permute-start
  238.5 3.7 collective-permute-done
  247.2 1.9 collective-permute-start
  249.2 3.7 collective-permute-done
  257.9 1.9 collective-permute-start
  259.8 3.7 collective-permute-done
  268.5 1.9 collective-permute-start
  270.4 3.7 collective-permute-done
  279.1 1.9 collective-permute-start
  281.1 3.7 collective-permute-done
  289.8 1.9 collective-permute-start
  291.7 3.7 collective-permute-done
  300.4 1.9 collective-permute-start
  302.3 3.7 collective-permute-done
  311.0 1.9 collective-permute-start
  313.0 3.7 collective-permute-done
  317.4 174.1 %while.38 = (s32[]{:T(128)}, bf16[4,8,8,128]{3,2,1,0:T(8,128)(2,1)}, f32[3456,128]{1,0:T(8,128)S(1)}, pred[]{:T(512)}, s32[]{:T(128)}, /*index=5*/bf16[8,4,8,8,1...) while((s32[]{:T(128)}, ...), condition=%wide.region_3.4_spmd.clone, body=%wide.region_2.3_spmd.clone.sunk | while | flops 457267200 | bytes 30126344 | solution.py:119
  322.7 3.1 collective-permute-start.1
  327.8 2.0 fusion.264
  335.2 4.8 collective-permute-start.1
  342.0 2.0 fusion.264
  353.3 2.0 fusion.264
  360.7 2.6 collective-permute-start.1
  365.3 2.0 fusion.264
  372.7 1.9 collective-permute-start.1
  376.6 2.0 fusion.264
  384.0 1.9 collective-permute-start.1
  387.9 2.0 fusion.264
  395.3 1.9 collective-permute-start.1
  399.2 2.0 fusion.264
  406.6 1.9 collective-permute-start.1
  410.5 2.0 fusion.264
  417.8 1.9 collective-permute-start.1
  421.8 2.0 fusion.264
  429.1 1.9 collective-permute-start.1
  433.1 2.0 fusion.264
  440.4 1.9 collective-permute-start.1
  444.4 2.0 fusion.264
  451.7 1.9 collective-permute-start.1
  455.6 2.0 fusion.264
  463.0 1.9 collective-permute-start.1
  466.9 2.0 fusion.264
  478.2 2.0 fusion.264
  489.5 2.0 fusion.264
  491.7 123.0 %fusion = bf16[112,128]{1,0:T(8,128)(2,1)S(1)} fusion(bf16[3456,128]{1,0:T(8,128)(2,1)S(1)} %convert_element_type.115), kind=kCustom, calls=%all-reduce-scatter | all-reduce-scatter fusion | flops 458753 | bytes 914432
  614.7 1.9 collective-permute-start.2
  616.6 1.9 collective-permute-start.3
  619.8 4.5 collective-permute-done.3
  (1116 shorter events, 193.7 us)
Async XLA Ops:
  162.1 5.6 collective-permute-start
  172.8 5.6 collective-permute-start
  183.4 5.6 collective-permute-start
  194.0 5.6 collective-permute-start
  204.7 5.6 collective-permute-start
  215.3 5.6 collective-permute-start
  226.0 5.6 collective-permute-start
  236.6 5.6 collective-permute-start
  247.2 5.6 collective-permute-start
  257.9 5.6 collective-permute-start
  268.5 5.6 collective-permute-start
  279.1 5.6 collective-permute-start
  289.8 5.6 collective-permute-start
  300.4 5.6 collective-permute-start
  311.0 5.6 collective-permute-start
  316.6 0.8 copy-start.1
  318.3 2.8 copy-start
  322.7 7.1 %collective-permute-start.1 = (bf16[4,8,8,128]{3,2,1,0:T(8,128)(2,1)}, bf16[4,8,8,128]{3,2,1,0:T(8,128)(2,1)}, u32[]{:S(2)}, u32[]{:S(2)}) collective-permute-start(bf16[4,8,8,128]{3,2,1,0:T(8,128)(2,1)} %get-tuple-element.632), channel_id=1, source_target_pairs={{32,0},{64,32},{96,64},{128,96},{160,128},{192,160},{224,192},{33,... | collective-permute-start | bytes 196616 | tf_op jit(solution)/shard_map/while/body/eval_jaxpr/ppermute | solution.py:10
  330.8 2.8 copy-start
  335.2 8.9 %collective-permute-start.1 = (bf16[4,8,8,128]{3,2,1,0:T(8,128)(2,1)}, bf16[4,8,8,128]{3,2,1,0:T(8,128)(2,1)}, u32[]{:S(2)}, u32[]{:S(2)}) collective-permute-start(bf16[4,8,8,128]{3,2,1,0:T(8,128)(2,1)} %get-tuple-element.632), channel_id=1, source_target_pairs={{32,0},{64,32},{96,64},{128,96},{160,128},{192,160},{224,192},{33,... | collective-permute-start | bytes 196616 | tf_op jit(solution)/shard_map/while/body/eval_jaxpr/ppermute | solution.py:10
  345.0 2.8 copy-start
  349.4 6.0 collective-permute-start.1
  356.3 2.8 copy-start
  360.7 6.7 %collective-permute-start.1 = (bf16[4,8,8,128]{3,2,1,0:T(8,128)(2,1)}, bf16[4,8,8,128]{3,2,1,0:T(8,128)(2,1)}, u32[]{:S(2)}, u32[]{:S(2)}) collective-permute-start(bf16[4,8,8,128]{3,2,1,0:T(8,128)(2,1)} %get-tuple-element.632), channel_id=1, source_target_pairs={{32,0},{64,32},{96,64},{128,96},{160,128},{192,160},{224,192},{33,... | collective-permute-start | bytes 196616 | tf_op jit(solution)/shard_map/while/body/eval_jaxpr/ppermute | solution.py:10
  368.3 2.8 copy-start
  372.7 6.0 collective-permute-start.1
  379.6 2.8 copy-start
  384.0 6.0 collective-permute-start.1
  390.9 2.8 copy-start
  395.3 6.0 collective-permute-start.1
  402.2 2.8 copy-start
  406.6 6.0 collective-permute-start.1
  413.4 2.8 copy-start
  417.8 6.0 collective-permute-start.1
  424.7 2.8 copy-start
  429.1 6.0 collective-permute-start.1
  436.0 2.8 copy-start
  440.4 6.0 collective-permute-start.1
  447.3 2.8 copy-start
  451.7 6.0 collective-permute-start.1
  458.6 2.8 copy-start
  463.0 6.0 collective-permute-start.1
  469.9 2.8 copy-start
  474.3 6.0 collective-permute-start.1
  481.2 2.8 copy-start
  485.6 6.0 collective-permute-start.1
  491.6 127.0 %copy-start.2 = (u32[256]{0:T(256)S(1)}, u32[256]{0:T(256)}, u32[]{:S(2)}) copy-start(u32[256]{0:T(256)} %constant.223) | copy-start | bytes 3076
  614.7 10.6 %collective-permute-start.2 = (bf16[112,128]{1,0:T(8,128)(2,1)S(1)}, bf16[112,128]{1,0:T(8,128)(2,1)S(1)}, u32[]{:S(2)}, u32[]{:S(2)}) collective-permute-start(bf16[112,128]{1,0:T(8,128)(2,1)S(1)} %fusion), channel_id=1, source_target_pairs={{0,1},{1,2},{2,3},{3,4},{4,5},{5,6},{6,7},{7,8},{8,9},{9,10},{10,1... | collective-permute-start | bytes 86024
  616.6 7.7 %collective-permute-start.3 = (bf16[12,128]{1,0:T(8,128)(2,1)S(1)}, bf16[12,128]{1,0:T(8,128)(2,1)S(1)}, u32[]{:S(2)}, u32[]{:S(2)}) collective-permute-start(bf16[12,128]{1,0:T(8,128)(2,1)S(1)} %slice.589), channel_id=1, source_target_pairs={{0,2},{1,3},{2,4},{3,5},{4,6},{5,7},{6,8},{7,9},{8,10},{9,11},{10,... | collective-permute-start | bytes 9224
where the time goes:
time: 633 us; the launch traced here: 626 us
  blocking collectives  276 us (44%)
  matrix products  85.5 us (14%)
  other arithmetic  82.8 us (13%)
  starting transfers between devices  66.2 us (10%)
  waiting for transfers between devices  60.3 us (10%)
  local copies, waits for them, and re-layouts  49.3 us (8%)
    all_gather x1, blocking collectives, per_device(): weight = lax.all_gather(weights, 'dp', axis=1, tiled=True)[0]  153 us
    unnamed x1, blocking collectives  123 us
    ppermute x30, starting transfers between devices, passed_along(): return lax.ppermute(block, axis, route)  62.3 us
    ppermute x30, waiting for transfers between devices, passed_along(): return lax.ppermute(block, axis, route)  54.8 us
    dot_general x15, matrix products, weight_term(): lax.dot_general(squash_columns(activation), flat_grad, (((0,), (0,)), (()...  30.6 us
    dot_general x15, matrix products, layer_forward(): jnp.dot(squash_columns(activation), weight, preferred_element_type=jnp.fl...  27.5 us
    dot_general x15, matrix products, input_gradient(): lax.dot_general(flat_grad, weight, (((1,), (1,)), ((), ())), preferred_el...  27.4 us
    convert_element_type x30, other arithmetic, squash_field(): return jax.nn.silu(activation.astype(jnp.float32)).astype(jnp.bfloat16)  23.9 us
  transfers between devices with their start and end apart: 32, of which 17 were waited for; matrix products, arithmetic and copies ran while one was open for 10% of the time, Pallas kernels for 0%

commit v1 on v0

--- a/solution.py
+++ b/solution.py
@@ -2,6 +2,135 @@
 import jax.numpy as jnp
 from jax import lax
 from jax.sharding import PartitionSpec as P
+
+from jax.experimental import pallas as pl
+from jax.experimental.pallas import tpu as pltpu
+
+MESH_ID = pl.DeviceIdType.MESH
+
+
+def greet_peers(peers, here, row):
+    barrier = pltpu.get_barrier_semaphore()
+
+    def signal(i, carry):
+        peer = lax.rem(here + i, peers)
+        pl.semaphore_signal(barrier, inc=1, device_id=(row, peer), device_id_type=MESH_ID)
+        return carry
+
+    lax.fori_loop(1, peers, signal, 0)
+    pl.semaphore_wait(barrier, peers - 1)
+
+
+def gather_kernel(shard_ref, out_ref, send_sem, recv_sem):
+    peers = lax.axis_size("dp")
+    here = lax.axis_index("dp")
+    row = lax.axis_index("section")
+    greet_peers(peers, here, row)
+
+    def outgoing(peer):
+        return pltpu.make_async_remote_copy(
+            src_ref=shard_ref,
+            dst_ref=out_ref.at[here],
+            send_sem=send_sem.at[peer],
+            recv_sem=recv_sem.at[here],
+            device_id=(row, peer),
+            device_id_type=MESH_ID,
+        )
+
+    def incoming(peer):
+        return pltpu.make_async_remote_copy(
+            src_ref=shard_ref,
+            dst_ref=out_ref.at[peer],
+            send_sem=send_sem.at[peer],
+            recv_sem=recv_sem.at[peer],
+            device_id=(row, peer),
+            device_id_type=MESH_ID,
+        )
+
+    def start(i, carry):
+        outgoing(lax.rem(here + i, peers)).start()
+        return carry
+
+    lax.fori_loop(1, peers, start, 0)
+    out_ref[here] = shard_ref[...]
+
+    def finish(i, carry):
+        peer = lax.rem(here + i, peers)
+        outgoing(peer).wait_send()
+        incoming(peer).wait_recv()
+        return carry
+
+    lax.fori_loop(1, peers, finish, 0)
+
+
+def gather_rows(shard):
+    peers = lax.axis_size("dp")
+    rows, cols = shard.shape
+    return pl.pallas_call(
+        gather_kernel,
+        out_shape=jax.ShapeDtypeStruct((peers, rows, cols), shard.dtype),
+        in_specs=[pl.BlockSpec(memory_space=pltpu.VMEM)],
+        out_specs=pl.BlockSpec(memory_space=pltpu.VMEM),
+        scratch_shapes=[pltpu.SemaphoreType.DMA((peers,)), pltpu.SemaphoreType.DMA((peers,))],
+        compiler_params=pltpu.CompilerParams(collective_id=0, has_side_effects=True),
+    )(shard)
+
+
+def scatter_kernel(parts_ref, out_ref, held, send_sem, recv_sem):
+    peers = lax.axis_size("dp")
+    here = lax.axis_index("dp")
+    row = lax.axis_index("section")
+    greet_peers(peers, here, row)
+
+    def outgoing(peer):
+        return pltpu.make_async_remote_copy(
+            src_ref=parts_ref.at[peer],
+            dst_ref=held.at[here],
+            send_sem=send_sem.at[peer],
+            recv_sem=recv_sem.at[here],
+            device_id=(row, peer),
+            device_id_type=MESH_ID,
+        )
+
+    def incoming(peer):
+        return pltpu.make_async_remote_copy(
+            src_ref=parts_ref.at[peer],
+            dst_ref=held.at[peer],
+            send_sem=send_sem.at[peer],
+            recv_sem=recv_sem.at[peer],
+            device_id=(row, peer),
+            device_id_type=MESH_ID,
+        )
+
+    def start(i, carry):
+        outgoing(lax.rem(here + i, peers)).start()
+        return carry
+
+    lax.fori_loop(1, peers, start, 0)
+
+    def finish(i, total):
+        peer = lax.rem(here + i, peers)
+        outgoing(peer).wait_send()
+        incoming(peer).wait_recv()
+        return total + held[peer]
+
+    out_ref[...] = lax.fori_loop(1, peers, finish, parts_ref[here])
+
+
+def scatter_rows(parts):
+    peers, rows, cols = parts.shape
+    return pl.pallas_call(
+        scatter_kernel,
+        out_shape=jax.ShapeDtypeStruct((rows, cols), parts.dtype),
+        in_specs=[pl.BlockSpec(memory_space=pltpu.VMEM)],
+        out_specs=pl.BlockSpec(memory_space=pltpu.VMEM),
+        scratch_shapes=[
+            pltpu.VMEM((peers, rows, cols), parts.dtype),
+            pltpu.SemaphoreType.DMA((peers,)),
+            pltpu.SemaphoreType.DMA((peers,)),
+        ],
+        compiler_params=pltpu.CompilerParams(collective_id=1, has_side_effects=True),
+    )(parts)
 
 
 def passed_along(block, axis, distance):
@@ -67,7 +196,7 @@
 def per_device(clips, cotangent, weights):
     section_total = lax.axis_size("section")
     section_index = lax.axis_index("section")
-    weight = lax.all_gather(weights, "dp", axis=1, tiled=True)[0]
+    weight = gather_rows(weights[0]).reshape(-1, weights.shape[-1])
     local_clips = clips[:, 0]
     local_grads = cotangent[:, 0]
     micro_count = local_clips.shape[0]
@@ -117,9 +246,7 @@
         jnp.zeros_like(local_grads),
     )
     _, grad_total, kept_grads = lax.fori_loop(0, step_count, backward_step, start_backward)
-    grad_share = lax.psum_scatter(
-        grad_total.astype(jnp.bfloat16), "dp", scatter_dimension=0, tiled=True
-    ).astype(jnp.float32)
+    grad_share = scatter_rows(grad_total.reshape(lax.axis_size("dp"), -1, grad_total.shape[-1]))
     return (produced[None, :, None], grad_share[None])
 
 

time: 633 us -> 432 us (0.68)
  the two profiles are of different devices: /device:TPU:98 before, /device:TPU:97 now
where the time goes in v1:
time: 432 us; the launch traced here: 425 us
  matrix products  85.5 us (20%)
  other arithmetic  82.4 us (19%)
  Pallas kernels  78.6 us (18%)
  waiting for transfers between devices  65.8 us (15%)
  starting transfers between devices  56.9 us (13%)
  local copies, waits for them, and re-layouts  51.3 us (12%)
    ppermute x30, waiting for transfers between devices, passed_along(): return lax.ppermute(block, axis, route)  65.8 us
    ppermute x30, starting transfers between devices, passed_along(): return lax.ppermute(block, axis, route)  56.9 us
    pallas_call x1, Pallas kernels, scatter_rows(): pl.pallas_call(scatter_kernel, out_shape=jax.ShapeDtypeStruct((rows, cols...  51.5 us
    dot_general x15, matrix products, weight_term(): lax.dot_general(squash_columns(activation), flat_grad, (((0,), (0,)), (()...  30.6 us
    dot_general x15, matrix products, layer_forward(): jnp.dot(squash_columns(activation), weight, preferred_element_type=jnp.fl...  27.5 us
    dot_general x15, matrix products, input_gradient(): lax.dot_general(flat_grad, weight, (((1,), (1,)), ((), ())), preferred_el...  27.4 us
    pallas_call x1, Pallas kernels, gather_rows(): pl.pallas_call(gather_kernel, out_shape=jax.ShapeDtypeStruct((peers, rows...  27.1 us
    convert_element_type x30, other arithmetic, squash_field(): return jax.nn.silu(activation.astype(jnp.float32)).astype(jnp.bfloat16)  24 us
  transfers between devices with their start and end apart: 30, of which 15 were waited for; matrix products, arithmetic and copies ran while one was open for 14% of the time, Pallas kernels for 0%

profile of v1, /device:TPU:97, one launch (start us, length us, event | category | flops | bytes accessed | tf_op | source)
XLA Modules:
  0.0 425.2 jit_solution(10281112575209471416)
XLA Ops:
  0.6 27.1 %shard_map.50 = bf16[32,108,128]{2,1,0:T(8,128)(2,1)} custom-call(bf16[108,128]{1,0:T(8,128)(2,1)} %bitcast.564), custom_call_target="tpu_custom_call" | custom-call | tf_op jit(solution)/shard_map/pallas_call | solution.py:69
  27.7 2.1 reshape.80
  30.9 161.1 %while.37 = (s32[]{:T(128)}, bf16[4,8,8,128]{3,2,1,0:T(8,128)(2,1)S(1)}, bf16[8,4,8,8,128]{4,3,2,1,0:T(8,128)(2,1)}, bf16[8,4,8,8,128]{4,3,2,1,0:T(8,128)(2,1)S(...) while((s32[]{:T(128)}, ...), condition=%wide.region_1.2_spmd, body=%wide.region_0.1_spmd.sunk | while | flops 227311616 | bytes 8454884 | solution.py:228
  37.3 5.1 %collective-permute-done = bf16[4,8,8,128]{3,2,1,0:T(8,128)(2,1)S(1)} collective-permute-done((bf16[4,8,8,128]{3,2,1,0:T(8,128)(2,1)S(1)}, bf16[4,8,8,128]{3,2,1,0:T(8,128)(2,1)S(1)}, u32[]{:S(2)}, u32[]{:S(2)}) %collective-permute-start) | collective-permute-done | bytes 65568 | tf_op jit(solution)/shard_map/while/body/eval_jaxpr/ppermute | solution.py:139
  45.6 1.8 bitcast_dynamic-update-slice_fusion.8
  48.7 5.0 %collective-permute-done = bf16[4,8,8,128]{3,2,1,0:T(8,128)(2,1)S(1)} collective-permute-done((bf16[4,8,8,128]{3,2,1,0:T(8,128)(2,1)S(1)}, bf16[4,8,8,128]{3,2,1,0:T(8,128)(2,1)S(1)}, u32[]{:S(2)}, u32[]{:S(2)}) %collective-permute-start) | collective-permute-done | bytes 65568 | tf_op jit(solution)/shard_map/while/body/eval_jaxpr/ppermute | solution.py:139
  57.0 1.8 bitcast_dynamic-update-slice_fusion.8
  60.1 4.3 %collective-permute-done = bf16[4,8,8,128]{3,2,1,0:T(8,128)(2,1)S(1)} collective-permute-done((bf16[4,8,8,128]{3,2,1,0:T(8,128)(2,1)S(1)}, bf16[4,8,8,128]{3,2,1,0:T(8,128)(2,1)S(1)}, u32[]{:S(2)}, u32[]{:S(2)}) %collective-permute-start) | collective-permute-done | bytes 65568 | tf_op jit(solution)/shard_map/while/body/eval_jaxpr/ppermute | solution.py:139
  67.6 1.8 bitcast_dynamic-update-slice_fusion.8
  70.7 4.3 %collective-permute-done = bf16[4,8,8,128]{3,2,1,0:T(8,128)(2,1)S(1)} collective-permute-done((bf16[4,8,8,128]{3,2,1,0:T(8,128)(2,1)S(1)}, bf16[4,8,8,128]{3,2,1,0:T(8,128)(2,1)S(1)}, u32[]{:S(2)}, u32[]{:S(2)}) %collective-permute-start) | collective-permute-done | bytes 65568 | tf_op jit(solution)/shard_map/while/body/eval_jaxpr/ppermute | solution.py:139
  78.2 1.8 bitcast_dynamic-update-slice_fusion.8
  81.4 4.3 %collective-permute-done = bf16[4,8,8,128]{3,2,1,0:T(8,128)(2,1)S(1)} collective-permute-done((bf16[4,8,8,128]{3,2,1,0:T(8,128)(2,1)S(1)}, bf16[4,8,8,128]{3,2,1,0:T(8,128)(2,1)S(1)}, u32[]{:S(2)}, u32[]{:S(2)}) %collective-permute-start) | collective-permute-done | bytes 65568 | tf_op jit(solution)/shard_map/while/body/eval_jaxpr/ppermute | solution.py:139
  88.9 1.8 bitcast_dynamic-update-slice_fusion.8
  92.0 4.3 %collective-permute-done = bf16[4,8,8,128]{3,2,1,0:T(8,128)(2,1)S(1)} collective-permute-done((bf16[4,8,8,128]{3,2,1,0:T(8,128)(2,1)S(1)}, bf16[4,8,8,128]{3,2,1,0:T(8,128)(2,1)S(1)}, u32[]{:S(2)}, u32[]{:S(2)}) %collective-permute-start) | collective-permute-done | bytes 65568 | tf_op jit(solution)/shard_map/while/body/eval_jaxpr/ppermute | solution.py:139
  99.5 1.8 bitcast_dynamic-update-slice_fusion.8
  102.6 4.3 %collective-permute-done = bf16[4,8,8,128]{3,2,1,0:T(8,128)(2,1)S(1)} collective-permute-done((bf16[4,8,8,128]{3,2,1,0:T(8,128)(2,1)S(1)}, bf16[4,8,8,128]{3,2,1,0:T(8,128)(2,1)S(1)}, u32[]{:S(2)}, u32[]{:S(2)}) %collective-permute-start) | collective-permute-done | bytes 65568 | tf_op jit(solution)/shard_map/while/body/eval_jaxpr/ppermute | solution.py:139
  110.1 1.8 bitcast_dynamic-update-slice_fusion.8
  113.3 4.3 %collective-permute-done = bf16[4,8,8,128]{3,2,1,0:T(8,128)(2,1)S(1)} collective-permute-done((bf16[4,8,8,128]{3,2,1,0:T(8,128)(2,1)S(1)}, bf16[4,8,8,128]{3,2,1,0:T(8,128)(2,1)S(1)}, u32[]{:S(2)}, u32[]{:S(2)}) %collective-permute-start) | collective-permute-done | bytes 65568 | tf_op jit(solution)/shard_map/while/body/eval_jaxpr/ppermute | solution.py:139
  120.8 1.8 bitcast_dynamic-update-slice_fusion.8
  123.9 4.3 %collective-permute-done = bf16[4,8,8,128]{3,2,1,0:T(8,128)(2,1)S(1)} collective-permute-done((bf16[4,8,8,128]{3,2,1,0:T(8,128)(2,1)S(1)}, bf16[4,8,8,128]{3,2,1,0:T(8,128)(2,1)S(1)}, u32[]{:S(2)}, u32[]{:S(2)}) %collective-permute-start) | collective-permute-done | bytes 65568 | tf_op jit(solution)/shard_map/while/body/eval_jaxpr/ppermute | solution.py:139
  131.4 1.8 bitcast_dynamic-update-slice_fusion.8
  134.6 4.3 %collective-permute-done = bf16[4,8,8,128]{3,2,1,0:T(8,128)(2,1)S(1)} collective-permute-done((bf16[4,8,8,128]{3,2,1,0:T(8,128)(2,1)S(1)}, bf16[4,8,8,128]{3,2,1,0:T(8,128)(2,1)S(1)}, u32[]{:S(2)}, u32[]{:S(2)}) %collective-permute-start) | collective-permute-done | bytes 65568 | tf_op jit(solution)/shard_map/while/body/eval_jaxpr/ppermute | solution.py:139
  142.0 1.8 bitcast_dynamic-update-slice_fusion.8
  145.2 4.3 %collective-permute-done = bf16[4,8,8,128]{3,2,1,0:T(8,128)(2,1)S(1)} collective-permute-done((bf16[4,8,8,128]{3,2,1,0:T(8,128)(2,1)S(1)}, bf16[4,8,8,128]{3,2,1,0:T(8,128)(2,1)S(1)}, u32[]{:S(2)}, u32[]{:S(2)}) %collective-permute-start) | collective-permute-done | bytes 65568 | tf_op jit(solution)/shard_map/while/body/eval_jaxpr/ppermute | solution.py:139
  152.7 1.8 bitcast_dynamic-update-slice_fusion.8
  155.8 4.3 %collective-permute-done = bf16[4,8,8,128]{3,2,1,0:T(8,128)(2,1)S(1)} collective-permute-done((bf16[4,8,8,128]{3,2,1,0:T(8,128)(2,1)S(1)}, bf16[4,8,8,128]{3,2,1,0:T(8,128)(2,1)S(1)}, u32[]{:S(2)}, u32[]{:S(2)}) %collective-permute-start) | collective-permute-done | bytes 65568 | tf_op jit(solution)/shard_map/while/body/eval_jaxpr/ppermute | solution.py:139
  163.3 1.8 bitcast_dynamic-update-slice_fusion.8
  166.5 4.3 %collective-permute-done = bf16[4,8,8,128]{3,2,1,0:T(8,128)(2,1)S(1)} collective-permute-done((bf16[4,8,8,128]{3,2,1,0:T(8,128)(2,1)S(1)}, bf16[4,8,8,128]{3,2,1,0:T(8,128)(2,1)S(1)}, u32[]{:S(2)}, u32[]{:S(2)}) %collective-permute-start) | collective-permute-done | bytes 65568 | tf_op jit(solution)/shard_map/while/body/eval_jaxpr/ppermute | solution.py:139
  174.0 1.8 bitcast_dynamic-update-slice_fusion.8
  177.1 4.3 %collective-permute-done = bf16[4,8,8,128]{3,2,1,0:T(8,128)(2,1)S(1)} collective-permute-done((bf16[4,8,8,128]{3,2,1,0:T(8,128)(2,1)S(1)}, bf16[4,8,8,128]{3,2,1,0:T(8,128)(2,1)S(1)}, u32[]{:S(2)}, u32[]{:S(2)}) %collective-permute-start) | collective-permute-done | bytes 65568 | tf_op jit(solution)/shard_map/while/body/eval_jaxpr/ppermute | solution.py:139
  184.6 1.8 bitcast_dynamic-update-slice_fusion.8
  187.7 4.3 %collective-permute-done = bf16[4,8,8,128]{3,2,1,0:T(8,128)(2,1)S(1)} collective-permute-done((bf16[4,8,8,128]{3,2,1,0:T(8,128)(2,1)S(1)}, bf16[4,8,8,128]{3,2,1,0:T(8,128)(2,1)S(1)}, u32[]{:S(2)}, u32[]{:S(2)}) %collective-permute-start) | collective-permute-done | bytes 65568 | tf_op jit(solution)/shard_map/while/body/eval_jaxpr/ppermute | solution.py:139
  193.5 177.3 %while.38 = (s32[]{:T(128)}, bf16[4,8,8,128]{3,2,1,0:T(8,128)(2,1)}, f32[3456,128]{1,0:T(8,128)S(1)}, pred[]{:T(512)}, s32[]{:T(128)}, /*index=5*/bf16[8,4,8,8,1...) while((s32[]{:T(128)}, ...), condition=%wide.region_3.4_spmd.clone, body=%wide.region_2.3_spmd.clone.sunk | while | flops 457267200 | bytes 30126344 | solution.py:248
  198.7 5.5 %collective-permute-start.1 = (bf16[4,8,8,128]{3,2,1,0:T(8,128)(2,1)}, bf16[4,8,8,128]{3,2,1,0:T(8,128)(2,1)}, u32[]{:S(2)}, u32[]{:S(2)}) collective-permute-start(bf16[4,8,8,128]{3,2,1,0:T(8,128)(2,1)} %get-tuple-element.632), channel_id=1, source_target_pairs={{32,0},{64,32},{96,64},{128,96},{160,128},{192,160},{224,192},{33,... | collective-permute-start | bytes 196616 | tf_op jit(solution)/shard_map/while/body/eval_jaxpr/ppermute | solution.py:139
  206.2 2.0 fusion.262
  213.5 2.3 collective-permute-start.1
  217.8 2.0 fusion.262
  225.1 4.9 %collective-permute-start.1 = (bf16[4,8,8,128]{3,2,1,0:T(8,128)(2,1)}, bf16[4,8,8,128]{3,2,1,0:T(8,128)(2,1)}, u32[]{:S(2)}, u32[]{:S(2)}) collective-permute-start(bf16[4,8,8,128]{3,2,1,0:T(8,128)(2,1)} %get-tuple-element.632), channel_id=1, source_target_pairs={{32,0},{64,32},{96,64},{128,96},{160,128},{192,160},{224,192},{33,... | collective-permute-start | bytes 196616 | tf_op jit(solution)/shard_map/while/body/eval_jaxpr/ppermute | solution.py:139
  232.0 2.0 fusion.262
  239.3 2.0 collective-permute-start.1
  243.3 2.0 fusion.262
  250.6 3.1 collective-permute-start.1
  255.7 2.0 fusion.262
  263.0 2.0 collective-permute-start.1
  267.0 2.0 fusion.262
  274.4 2.0 collective-permute-start.1
  278.3 2.0 fusion.262
  285.7 2.0 collective-permute-start.1
  289.6 2.0 fusion.262
  297.0 2.0 collective-permute-start.1
  300.9 2.0 fusion.262
  308.3 2.0 collective-permute-start.1
  312.2 2.0 fusion.262
  319.6 2.0 collective-permute-start.1
  323.5 2.0 fusion.262
  330.9 2.0 collective-permute-start.1
  334.8 2.0 fusion.262
  342.2 2.0 collective-permute-start.1
  346.1 2.0 fusion.262
  353.5 2.0 collective-permute-start.1
  357.4 2.0 fusion.262
  364.8 2.0 collective-permute-start.1
  368.7 2.0 fusion.262
  372.2 51.5 %shard_map.51 = f32[108,128]{1,0:T(8,128)} custom-call(f32[32,108,128]{2,1,0:T(8,128)} %reshape.81.parts_ref), custom_call_target="tpu_custom_call" | custom-call | tf_op jit(solution)/shard_map/pallas_call | solution.py:122
  (1105 shorter events, 180.2 us)
Async XLA Ops:
  36.0 6.4 %collective-permute-start = (bf16[4,8,8,128]{3,2,1,0:T(8,128)(2,1)S(1)}, bf16[4,8,8,128]{3,2,1,0:T(8,128)(2,1)S(1)}, u32[]{:S(2)}, u32[]{:S(2)}) collective-permute-start(bf16[4,8,8,128]{3,2,1,0:T(8,128)(2,1)S(1)} %get-tuple-element.594), channel_id=1, source_target_pairs={{0,32},{32,64},{64,96},{96,128},{128,160},{160,192},{192,224},{1,3... | collective-permute-start | bytes 196616 | tf_op jit(solution)/shard_map/while/body/eval_jaxpr/ppermute | solution.py:139
  47.4 6.3 %collective-permute-start = (bf16[4,8,8,128]{3,2,1,0:T(8,128)(2,1)S(1)}, bf16[4,8,8,128]{3,2,1,0:T(8,128)(2,1)S(1)}, u32[]{:S(2)}, u32[]{:S(2)}) collective-permute-start(bf16[4,8,8,128]{3,2,1,0:T(8,128)(2,1)S(1)} %get-tuple-element.594), channel_id=1, source_target_pairs={{0,32},{32,64},{64,96},{96,128},{128,160},{160,192},{192,224},{1,3... | collective-permute-start | bytes 196616 | tf_op jit(solution)/shard_map/while/body/eval_jaxpr/ppermute | solution.py:139
  58.8 5.6 %collective-permute-start = (bf16[4,8,8,128]{3,2,1,0:T(8,128)(2,1)S(1)}, bf16[4,8,8,128]{3,2,1,0:T(8,128)(2,1)S(1)}, u32[]{:S(2)}, u32[]{:S(2)}) collective-permute-start(bf16[4,8,8,128]{3,2,1,0:T(8,128)(2,1)S(1)} %get-tuple-element.594), channel_id=1, source_target_pairs={{0,32},{32,64},{64,96},{96,128},{128,160},{160,192},{192,224},{1,3... | collective-permute-start | bytes 196616 | tf_op jit(solution)/shard_map/while/body/eval_jaxpr/ppermute | solution.py:139
  69.4 5.6 %collective-permute-start = (bf16[4,8,8,128]{3,2,1,0:T(8,128)(2,1)S(1)}, bf16[4,8,8,128]{3,2,1,0:T(8,128)(2,1)S(1)}, u32[]{:S(2)}, u32[]{:S(2)}) collective-permute-start(bf16[4,8,8,128]{3,2,1,0:T(8,128)(2,1)S(1)} %get-tuple-element.594), channel_id=1, source_target_pairs={{0,32},{32,64},{64,96},{96,128},{128,160},{160,192},{192,224},{1,3... | collective-permute-start | bytes 196616 | tf_op jit(solution)/shard_map/while/body/eval_jaxpr/ppermute | solution.py:139
  80.1 5.6 %collective-permute-start = (bf16[4,8,8,128]{3,2,1,0:T(8,128)(2,1)S(1)}, bf16[4,8,8,128]{3,2,1,0:T(8,128)(2,1)S(1)}, u32[]{:S(2)}, u32[]{:S(2)}) collective-permute-start(bf16[4,8,8,128]{3,2,1,0:T(8,128)(2,1)S(1)} %get-tuple-element.594), channel_id=1, source_target_pairs={{0,32},{32,64},{64,96},{96,128},{128,160},{160,192},{192,224},{1,3... | collective-permute-start | bytes 196616 | tf_op jit(solution)/shard_map/while/body/eval_jaxpr/ppermute | solution.py:139
  90.7 5.6 %collective-permute-start = (bf16[4,8,8,128]{3,2,1,0:T(8,128)(2,1)S(1)}, bf16[4,8,8,128]{3,2,1,0:T(8,128)(2,1)S(1)}, u32[]{:S(2)}, u32[]{:S(2)}) collective-permute-start(bf16[4,8,8,128]{3,2,1,0:T(8,128)(2,1)S(1)} %get-tuple-element.594), channel_id=1, source_target_pairs={{0,32},{32,64},{64,96},{96,128},{128,160},{160,192},{192,224},{1,3... | collective-permute-start | bytes 196616 | tf_op jit(solution)/shard_map/while/body/eval_jaxpr/ppermute | solution.py:139
  101.3 5.6 %collective-permute-start = (bf16[4,8,8,128]{3,2,1,0:T(8,128)(2,1)S(1)}, bf16[4,8,8,128]{3,2,1,0:T(8,128)(2,1)S(1)}, u32[]{:S(2)}, u32[]{:S(2)}) collective-permute-start(bf16[4,8,8,128]{3,2,1,0:T(8,128)(2,1)S(1)} %get-tuple-element.594), channel_id=1, source_target_pairs={{0,32},{32,64},{64,96},{96,128},{128,160},{160,192},{192,224},{1,3... | collective-permute-start | bytes 196616 | tf_op jit(solution)/shard_map/while/body/eval_jaxpr/ppermute | solution.py:139
  112.0 5.6 %collective-permute-start = (bf16[4,8,8,128]{3,2,1,0:T(8,128)(2,1)S(1)}, bf16[4,8,8,128]{3,2,1,0:T(8,128)(2,1)S(1)}, u32[]{:S(2)}, u32[]{:S(2)}) collective-permute-start(bf16[4,8,8,128]{3,2,1,0:T(8,128)(2,1)S(1)} %get-tuple-element.594), channel_id=1, source_target_pairs={{0,32},{32,64},{64,96},{96,128},{128,160},{160,192},{192,224},{1,3... | collective-permute-start | bytes 196616 | tf_op jit(solution)/shard_map/while/body/eval_jaxpr/ppermute | solution.py:139
  122.6 5.6 %collective-permute-start = (bf16[4,8,8,128]{3,2,1,0:T(8,128)(2,1)S(1)}, bf16[4,8,8,128]{3,2,1,0:T(8,128)(2,1)S(1)}, u32[]{:S(2)}, u32[]{:S(2)}) collective-permute-start(bf16[4,8,8,128]{3,2,1,0:T(8,128)(2,1)S(1)} %get-tuple-element.594), channel_id=1, source_target_pairs={{0,32},{32,64},{64,96},{96,128},{128,160},{160,192},{192,224},{1,3... | collective-permute-start | bytes 196616 | tf_op jit(solution)/shard_map/while/body/eval_jaxpr/ppermute | solution.py:139
  133.3 5.6 %collective-permute-start = (bf16[4,8,8,128]{3,2,1,0:T(8,128)(2,1)S(1)}, bf16[4,8,8,128]{3,2,1,0:T(8,128)(2,1)S(1)}, u32[]{:S(2)}, u32[]{:S(2)}) collective-permute-start(bf16[4,8,8,128]{3,2,1,0:T(8,128)(2,1)S(1)} %get-tuple-element.594), channel_id=1, source_target_pairs={{0,32},{32,64},{64,96},{96,128},{128,160},{160,192},{192,224},{1,3... | collective-permute-start | bytes 196616 | tf_op jit(solution)/shard_map/while/body/eval_jaxpr/ppermute | solution.py:139
  143.9 5.6 %collective-permute-start = (bf16[4,8,8,128]{3,2,1,0:T(8,128)(2,1)S(1)}, bf16[4,8,8,128]{3,2,1,0:T(8,128)(2,1)S(1)}, u32[]{:S(2)}, u32[]{:S(2)}) collective-permute-start(bf16[4,8,8,128]{3,2,1,0:T(8,128)(2,1)S(1)} %get-tuple-element.594), channel_id=1, source_target_pairs={{0,32},{32,64},{64,96},{96,128},{128,160},{160,192},{192,224},{1,3... | collective-permute-start | bytes 196616 | tf_op jit(solution)/shard_map/while/body/eval_jaxpr/ppermute | solution.py:139
  154.5 5.6 %collective-permute-start = (bf16[4,8,8,128]{3,2,1,0:T(8,128)(2,1)S(1)}, bf16[4,8,8,128]{3,2,1,0:T(8,128)(2,1)S(1)}, u32[]{:S(2)}, u32[]{:S(2)}) collective-permute-start(bf16[4,8,8,128]{3,2,1,0:T(8,128)(2,1)S(1)} %get-tuple-element.594), channel_id=1, source_target_pairs={{0,32},{32,64},{64,96},{96,128},{128,160},{160,192},{192,224},{1,3... | collective-permute-start | bytes 196616 | tf_op jit(solution)/shard_map/while/body/eval_jaxpr/ppermute | solution.py:139
  165.2 5.6 %collective-permute-start = (bf16[4,8,8,128]{3,2,1,0:T(8,128)(2,1)S(1)}, bf16[4,8,8,128]{3,2,1,0:T(8,128)(2,1)S(1)}, u32[]{:S(2)}, u32[]{:S(2)}) collective-permute-start(bf16[4,8,8,128]{3,2,1,0:T(8,128)(2,1)S(1)} %get-tuple-element.594), channel_id=1, source_target_pairs={{0,32},{32,64},{64,96},{96,128},{128,160},{160,192},{192,224},{1,3... | collective-permute-start | bytes 196616 | tf_op jit(solution)/shard_map/while/body/eval_jaxpr/ppermute | solution.py:139
  175.8 5.6 %collective-permute-start = (bf16[4,8,8,128]{3,2,1,0:T(8,128)(2,1)S(1)}, bf16[4,8,8,128]{3,2,1,0:T(8,128)(2,1)S(1)}, u32[]{:S(2)}, u32[]{:S(2)}) collective-permute-start(bf16[4,8,8,128]{3,2,1,0:T(8,128)(2,1)S(1)} %get-tuple-element.594), channel_id=1, source_target_pairs={{0,32},{32,64},{64,96},{96,128},{128,160},{160,192},{192,224},{1,3... | collective-permute-start | bytes 196616 | tf_op jit(solution)/shard_map/while/body/eval_jaxpr/ppermute | solution.py:139
  186.4 5.6 %collective-permute-start = (bf16[4,8,8,128]{3,2,1,0:T(8,128)(2,1)S(1)}, bf16[4,8,8,128]{3,2,1,0:T(8,128)(2,1)S(1)}, u32[]{:S(2)}, u32[]{:S(2)}) collective-permute-start(bf16[4,8,8,128]{3,2,1,0:T(8,128)(2,1)S(1)} %get-tuple-element.594), channel_id=1, source_target_pairs={{0,32},{32,64},{64,96},{96,128},{128,160},{160,192},{192,224},{1,3... | collective-permute-start | bytes 196616 | tf_op jit(solution)/shard_map/while/body/eval_jaxpr/ppermute | solution.py:139
  192.0 0.8 copy-start.1
  194.3 2.8 copy-start
  198.7 9.5 %collective-permute-start.1 = (bf16[4,8,8,128]{3,2,1,0:T(8,128)(2,1)}, bf16[4,8,8,128]{3,2,1,0:T(8,128)(2,1)}, u32[]{:S(2)}, u32[]{:S(2)}) collective-permute-start(bf16[4,8,8,128]{3,2,1,0:T(8,128)(2,1)} %get-tuple-element.632), channel_id=1, source_target_pairs={{32,0},{64,32},{96,64},{128,96},{160,128},{192,160},{224,192},{33,... | collective-permute-start | bytes 196616 | tf_op jit(solution)/shard_map/while/body/eval_jaxpr/ppermute | solution.py:139
  209.1 2.8 copy-start
  213.5 6.3 %collective-permute-start.1 = (bf16[4,8,8,128]{3,2,1,0:T(8,128)(2,1)}, bf16[4,8,8,128]{3,2,1,0:T(8,128)(2,1)}, u32[]{:S(2)}, u32[]{:S(2)}) collective-permute-start(bf16[4,8,8,128]{3,2,1,0:T(8,128)(2,1)} %get-tuple-element.632), channel_id=1, source_target_pairs={{32,0},{64,32},{96,64},{128,96},{160,128},{192,160},{224,192},{33,... | collective-permute-start | bytes 196616 | tf_op jit(solution)/shard_map/while/body/eval_jaxpr/ppermute | solution.py:139
  220.7 2.8 copy-start
  225.1 8.9 %collective-permute-start.1 = (bf16[4,8,8,128]{3,2,1,0:T(8,128)(2,1)}, bf16[4,8,8,128]{3,2,1,0:T(8,128)(2,1)}, u32[]{:S(2)}, u32[]{:S(2)}) collective-permute-start(bf16[4,8,8,128]{3,2,1,0:T(8,128)(2,1)} %get-tuple-element.632), channel_id=1, source_target_pairs={{32,0},{64,32},{96,64},{128,96},{160,128},{192,160},{224,192},{33,... | collective-permute-start | bytes 196616 | tf_op jit(solution)/shard_map/while/body/eval_jaxpr/ppermute | solution.py:139
  234.9 2.8 copy-start
  239.3 6.0 %collective-permute-start.1 = (bf16[4,8,8,128]{3,2,1,0:T(8,128)(2,1)}, bf16[4,8,8,128]{3,2,1,0:T(8,128)(2,1)}, u32[]{:S(2)}, u32[]{:S(2)}) collective-permute-start(bf16[4,8,8,128]{3,2,1,0:T(8,128)(2,1)} %get-tuple-element.632), channel_id=1, source_target_pairs={{32,0},{64,32},{96,64},{128,96},{160,128},{192,160},{224,192},{33,... | collective-permute-start | bytes 196616 | tf_op jit(solution)/shard_map/while/body/eval_jaxpr/ppermute | solution.py:139
  246.2 2.8 copy-start
  250.6 7.1 %collective-permute-start.1 = (bf16[4,8,8,128]{3,2,1,0:T(8,128)(2,1)}, bf16[4,8,8,128]{3,2,1,0:T(8,128)(2,1)}, u32[]{:S(2)}, u32[]{:S(2)}) collective-permute-start(bf16[4,8,8,128]{3,2,1,0:T(8,128)(2,1)} %get-tuple-element.632), channel_id=1, source_target_pairs={{32,0},{64,32},{96,64},{128,96},{160,128},{192,160},{224,192},{33,... | collective-permute-start | bytes 196616 | tf_op jit(solution)/shard_map/while/body/eval_jaxpr/ppermute | solution.py:139
  258.6 2.8 copy-start
  263.0 6.0 %collective-permute-start.1 = (bf16[4,8,8,128]{3,2,1,0:T(8,128)(2,1)}, bf16[4,8,8,128]{3,2,1,0:T(8,128)(2,1)}, u32[]{:S(2)}, u32[]{:S(2)}) collective-permute-start(bf16[4,8,8,128]{3,2,1,0:T(8,128)(2,1)} %get-tuple-element.632), channel_id=1, source_target_pairs={{32,0},{64,32},{96,64},{128,96},{160,128},{192,160},{224,192},{33,... | collective-permute-start | bytes 196616 | tf_op jit(solution)/shard_map/while/body/eval_jaxpr/ppermute | solution.py:139
  269.9 2.8 copy-start
  274.4 6.0 %collective-permute-start.1 = (bf16[4,8,8,128]{3,2,1,0:T(8,128)(2,1)}, bf16[4,8,8,128]{3,2,1,0:T(8,128)(2,1)}, u32[]{:S(2)}, u32[]{:S(2)}) collective-permute-start(bf16[4,8,8,128]{3,2,1,0:T(8,128)(2,1)} %get-tuple-element.632), channel_id=1, source_target_pairs={{32,0},{64,32},{96,64},{128,96},{160,128},{192,160},{224,192},{33,... | collective-permute-start | bytes 196616 | tf_op jit(solution)/shard_map/while/body/eval_jaxpr/ppermute | solution.py:139
  281.3 2.8 copy-start
  285.7 6.0 %collective-permute-start.1 = (bf16[4,8,8,128]{3,2,1,0:T(8,128)(2,1)}, bf16[4,8,8,128]{3,2,1,0:T(8,128)(2,1)}, u32[]{:S(2)}, u32[]{:S(2)}) collective-permute-start(bf16[4,8,8,128]{3,2,1,0:T(8,128)(2,1)} %get-tuple-element.632), channel_id=1, source_target_pairs={{32,0},{64,32},{96,64},{128,96},{160,128},{192,160},{224,192},{33,... | collective-permute-start | bytes 196616 | tf_op jit(solution)/shard_map/while/body/eval_jaxpr/ppermute | solution.py:139
  292.5 2.8 copy-start
  297.0 6.0 %collective-permute-start.1 = (bf16[4,8,8,128]{3,2,1,0:T(8,128)(2,1)}, bf16[4,8,8,128]{3,2,1,0:T(8,128)(2,1)}, u32[]{:S(2)}, u32[]{:S(2)}) collective-permute-start(bf16[4,8,8,128]{3,2,1,0:T(8,128)(2,1)} %get-tuple-element.632), channel_id=1, source_target_pairs={{32,0},{64,32},{96,64},{128,96},{160,128},{192,160},{224,192},{33,... | collective-permute-start | bytes 196616 | tf_op jit(solution)/shard_map/while/body/eval_jaxpr/ppermute | solution.py:139
  303.8 2.8 copy-start
  308.3 6.0 %collective-permute-start.1 = (bf16[4,8,8,128]{3,2,1,0:T(8,128)(2,1)}, bf16[4,8,8,128]{3,2,1,0:T(8,128)(2,1)}, u32[]{:S(2)}, u32[]{:S(2)}) collective-permute-start(bf16[4,8,8,128]{3,2,1,0:T(8,128)(2,1)} %get-tuple-element.632), channel_id=1, source_target_pairs={{32,0},{64,32},{96,64},{128,96},{160,128},{192,160},{224,192},{33,... | collective-permute-start | bytes 196616 | tf_op jit(solution)/shard_map/while/body/eval_jaxpr/ppermute | solution.py:139
  315.1 2.8 copy-start
  319.6 6.0 %collective-permute-start.1 = (bf16[4,8,8,128]{3,2,1,0:T(8,128)(2,1)}, bf16[4,8,8,128]{3,2,1,0:T(8,128)(2,1)}, u32[]{:S(2)}, u32[]{:S(2)}) collective-permute-start(bf16[4,8,8,128]{3,2,1,0:T(8,128)(2,1)} %get-tuple-element.632), channel_id=1, source_target_pairs={{32,0},{64,32},{96,64},{128,96},{160,128},{192,160},{224,192},{33,... | collective-permute-start | bytes 196616 | tf_op jit(solution)/shard_map/while/body/eval_jaxpr/ppermute | solution.py:139
  326.5 2.8 copy-start
  330.9 6.0 %collective-permute-start.1 = (bf16[4,8,8,128]{3,2,1,0:T(8,128)(2,1)}, bf16[4,8,8,128]{3,2,1,0:T(8,128)(2,1)}, u32[]{:S(2)}, u32[]{:S(2)}) collective-permute-start(bf16[4,8,8,128]{3,2,1,0:T(8,128)(2,1)} %get-tuple-element.632), channel_id=1, source_target_pairs={{32,0},{64,32},{96,64},{128,96},{160,128},{192,160},{224,192},{33,... | collective-permute-start | bytes 196616 | tf_op jit(solution)/shard_map/while/body/eval_jaxpr/ppermute | solution.py:139
  337.8 2.8 copy-start
  342.2 6.0 %collective-permute-start.1 = (bf16[4,8,8,128]{3,2,1,0:T(8,128)(2,1)}, bf16[4,8,8,128]{3,2,1,0:T(8,128)(2,1)}, u32[]{:S(2)}, u32[]{:S(2)}) collective-permute-start(bf16[4,8,8,128]{3,2,1,0:T(8,128)(2,1)} %get-tuple-element.632), channel_id=1, source_target_pairs={{32,0},{64,32},{96,64},{128,96},{160,128},{192,160},{224,192},{33,... | collective-permute-start | bytes 196616 | tf_op jit(solution)/shard_map/while/body/eval_jaxpr/ppermute | solution.py:139
  349.1 2.8 copy-start
  353.5 6.0 %collective-permute-start.1 = (bf16[4,8,8,128]{3,2,1,0:T(8,128)(2,1)}, bf16[4,8,8,128]{3,2,1,0:T(8,128)(2,1)}, u32[]{:S(2)}, u32[]{:S(2)}) collective-permute-start(bf16[4,8,8,128]{3,2,1,0:T(8,128)(2,1)} %get-tuple-element.632), channel_id=1, source_target_pairs={{32,0},{64,32},{96,64},{128,96},{160,128},{192,160},{224,192},{33,... | collective-permute-start | bytes 196616 | tf_op jit(solution)/shard_map/while/body/eval_jaxpr/ppermute | solution.py:139
  360.4 2.8 copy-start
  364.8 6.0 %collective-permute-start.1 = (bf16[4,8,8,128]{3,2,1,0:T(8,128)(2,1)}, bf16[4,8,8,128]{3,2,1,0:T(8,128)(2,1)}, u32[]{:S(2)}, u32[]{:S(2)}) collective-permute-start(bf16[4,8,8,128]{3,2,1,0:T(8,128)(2,1)} %get-tuple-element.632), channel_id=1, source_target_pairs={{32,0},{64,32},{96,64},{128,96},{160,128},{192,160},{224,192},{33,... | collective-permute-start | bytes 196616 | tf_op jit(solution)/shard_map/while/body/eval_jaxpr/ppermute | solution.py:139

commit v2 on v1

v2 whole, which is shorter than its diff:
```python
import jax
import jax.numpy as jnp
from jax import lax
from jax.sharding import PartitionSpec as P

from jax.experimental import pallas as pl
from jax.experimental.pallas import tpu as pltpu

MESH_ID = pl.DeviceIdType.MESH


def greet_peers(peers, here, row):
    barrier = pltpu.get_barrier_semaphore()

    def signal(i, carry):
        peer = lax.rem(here + i, peers)
        pl.semaphore_signal(barrier, inc=1, device_id=(row, peer), device_id_type=MESH_ID)
        return carry

    lax.fori_loop(1, peers, signal, 0)
    pl.semaphore_wait(barrier, peers - 1)


def gather_kernel(shard_ref, out_ref, send_sem, recv_sem):
    peers = lax.axis_size("dp")
    here = lax.axis_index("dp")
    row = lax.axis_index("section")
    greet_peers(peers, here, row)

    def outgoing(peer):
        return pltpu.make_async_remote_copy(
            src_ref=shard_ref,
            dst_ref=out_ref.at[here],
            send_sem=send_sem.at[peer],
            recv_sem=recv_sem.at[here],
            device_id=(row, peer),
            device_id_type=MESH_ID,
        )

    def incoming(peer):
        return pltpu.make_async_remote_copy(
            src_ref=shard_ref,
            dst_ref=out_ref.at[peer],
            send_sem=send_sem.at[peer],
            recv_sem=recv_sem.at[peer],
            device_id=(row, peer),
            device_id_type=MESH_ID,
        )

    def start(i, carry):
        outgoing(lax.rem(here + i, peers)).start()
        return carry

    lax.fori_loop(1, peers, start, 0)
    out_ref[here] = shard_ref[...]

    def finish(i, carry):
        peer = lax.rem(here + i, peers)
        outgoing(peer).wait_send()
        incoming(peer).wait_recv()
        return carry

    lax.fori_loop(1, peers, finish, 0)


def gather_rows(shard):
    peers = lax.axis_size("dp")
    rows, cols = shard.shape
    return pl.pallas_call(
        gather_kernel,
        out_shape=jax.ShapeDtypeStruct((peers, rows, cols), shard.dtype),
        in_specs=[pl.BlockSpec(memory_space=pltpu.VMEM)],
        out_specs=pl.BlockSpec(memory_space=pltpu.VMEM),
        scratch_shapes=[pltpu.SemaphoreType.DMA((peers,)), pltpu.SemaphoreType.DMA((peers,))],
        compiler_params=pltpu.CompilerParams(collective_id=0, has_side_effects=True),
    )(shard)


def scatter_kernel(parts_ref, out_ref, held, send_sem, recv_sem):
    peers = lax.axis_size("dp")
    here = lax.axis_index("dp")
    row = lax.axis_index("section")
    greet_peers(peers, here, row)

    def outgoing(peer):
        return pltpu.make_async_remote_copy(
            src_ref=parts_ref.at[peer],
            dst_ref=held.at[here],
            send_sem=send_sem.at[peer],
            recv_sem=recv_sem.at[here],
            device_id=(row, peer),
            device_id_type=MESH_ID,
        )

    def incoming(peer):
        return pltpu.make_async_remote_copy(
            src_ref=parts_ref.at[peer],
            dst_ref=held.at[peer],
            send_sem=send_sem.at[peer],
            recv_sem=recv_sem.at[peer],
            device_id=(row, peer),
            device_id_type=MESH_ID,
        )

    def start(i, carry):
        outgoing(lax.rem(here + i, peers)).start()
        return carry

    lax.fori_loop(1, peers, start, 0)

    def finish(i, total):
        peer = lax.rem(here + i, peers)
        outgoing(peer).wait_send()
        incoming(peer).wait_recv()
        return total + held[peer]

    out_ref[...] = lax.fori_loop(1, peers, finish, parts_ref[here])


def scatter_rows(parts):
    peers, rows, cols = parts.shape
    return pl.pallas_call(
        scatter_kernel,
        out_shape=jax.ShapeDtypeStruct((rows, cols), parts.dtype),
        in_specs=[pl.BlockSpec(memory_space=pltpu.VMEM)],
        out_specs=pl.BlockSpec(memory_space=pltpu.VMEM),
        scratch_shapes=[
            pltpu.VMEM((peers, rows, cols), parts.dtype),
            pltpu.SemaphoreType.DMA((peers,)),
            pltpu.SemaphoreType.DMA((peers,)),
        ],
        compiler_params=pltpu.CompilerParams(collective_id=1, has_side_effects=True),
    )(parts)


def squash_into(pad_ref, activation):
    squashed = (activation / (1.0 + jnp.exp(-activation))).astype(jnp.bfloat16).astype(jnp.float32)
    field = squashed.reshape(pad_ref.shape[0] - 2, 8, 8, pad_ref.shape[-1])
    pad_ref[2:, 1:9, 1:9, :] = field
    pad_ref[0:2, 1:9, 1:9, :] = jnp.broadcast_to(field[0:1], (2,) + field.shape[1:])


def tap_window(pad_ref, tap, frames, base):
    offset_time, offset_row, offset_col = tap // 9, (tap // 3) % 3, tap % 3
    if base:
        t0, r0, c0 = 2 - offset_time, 2 - offset_row, 2 - offset_col
    else:
        t0, r0, c0 = offset_time, offset_row, offset_col
    window = pad_ref[t0 : t0 + frames, r0 : r0 + 8, c0 : c0 + 8, :]
    return window.reshape(frames * 64, window.shape[-1]).astype(jnp.bfloat16)


def greet_line(here, count, col):
    barrier = pltpu.get_barrier_semaphore()

    @pl.when(here > 0)
    def _():
        pl.semaphore_signal(barrier, inc=1, device_id=(here - 1, col), device_id_type=MESH_ID)

    @pl.when(here < count - 1)
    def _():
        pl.semaphore_signal(barrier, inc=1, device_id=(here + 1, col), device_id_type=MESH_ID)

    neighbours = (here + count - 1) // count + (2 * count - 2 - here) // count
    pl.semaphore_wait(barrier, neighbours)


def line_copy(src, dst, send_sem, recv_sem, target, col):
    return pltpu.make_async_remote_copy(
        src_ref=src,
        dst_ref=dst,
        send_sem=send_sem,
        recv_sem=recv_sem,
        device_id=(target, col),
        device_id_type=MESH_ID,
    )


def forward_kernel(clips_ref, w_ref, seen_ref, out_ref, recv, pad, send_sem, recv_sem):
    count = lax.axis_size("section")
    here = lax.axis_index("section")
    col = lax.axis_index("dp")
    micro_count = clips_ref.shape[0]
    greet_line(here, count, col)
    pad[...] = jnp.zeros_like(pad)

    def step(m, carry):
        @pl.when(here == 0)
        def _():
            seen_ref[m] = clips_ref[m]

        @pl.when(here > 0)
        def _():
            line_copy(out_ref.at[m], recv.at[m], send_sem.at[m], recv_sem.at[m], here - 1, col).wait_recv()
            seen_ref[m] = recv[m]

        base = seen_ref[m].astype(jnp.float32)
        squash_into(pad, base)
        total = base
        for tap in range(27):
            total = total + jnp.dot(tap_window(pad, tap, 4, False), w_ref[tap], preferred_element_type=jnp.float32)
        out_ref[m] = total.astype(out_ref.dtype)

        @pl.when(here < count - 1)
        def _():
            line_copy(out_ref.at[m], recv.at[m], send_sem.at[m], recv_sem.at[m], here + 1, col).start()

        return carry

    lax.fori_loop(0, micro_count, step, 0)

    @pl.when(here < count - 1)
    def _():
        for m in range(micro_count):
            line_copy(out_ref.at[m], recv.at[m], send_sem.at[m], recv_sem.at[m], here + 1, col).wait_send()


def forward_line(clips_local, weight):
    shape = jax.ShapeDtypeStruct(clips_local.shape, clips_local.dtype)
    micro_count, cells, channels = clips_local.shape
    return pl.pallas_call(
        forward_kernel,
        out_shape=(shape, shape),
        in_specs=[pl.BlockSpec(memory_space=pltpu.VMEM)] * 2,
        out_specs=(pl.BlockSpec(memory_space=pltpu.VMEM),) * 2,
        scratch_shapes=[
            pltpu.VMEM(clips_local.shape, clips_local.dtype),
            pltpu.VMEM((cells // 64 + 2, 10, 10, channels), jnp.float32),
            pltpu.SemaphoreType.DMA((micro_count,)),
            pltpu.SemaphoreType.DMA((micro_count,)),
        ],
        compiler_params=pltpu.CompilerParams(collective_id=2, has_side_effects=True),
    )(clips_local, weight)


def backward_kernel(cot_ref, seen_ref, w_ref, wg_ref, recv, sendbuf, pad, gpad, send_sem, recv_sem):
    count = lax.axis_size("section")
    here = lax.axis_index("section")
    col = lax.axis_index("dp")
    micro_count = cot_ref.shape[0]
    greet_line(here, count, col)
    pad[...] = jnp.zeros_like(pad)
    gpad[...] = jnp.zeros_like(gpad)
    wg_ref[...] = jnp.zeros_like(wg_ref)

    def step(m, carry):
        @pl.when(here == count - 1)
        def _():
            recv[m] = cot_ref[m]

        @pl.when(here < count - 1)
        def _():
            line_copy(sendbuf.at[m], recv.at[m], send_sem.at[m], recv_sem.at[m], here + 1, col).wait_recv()

        upstream = recv[m]
        base = seen_ref[m].astype(jnp.float32)
        squash_into(pad, base)
        for tap in range(27):
            wg_ref[tap] += lax.dot_general(
                tap_window(pad, tap, 4, False), upstream, (((0,), (0,)), ((), ())),
                preferred_element_type=jnp.float32,
            )

        @pl.when(here > 0)
        def _():
            up = upstream.astype(jnp.float32)
            gpad[2:6, 1:9, 1:9, :] = up.reshape(4, 8, 8, up.shape[-1])
            spread = jnp.zeros((384, up.shape[-1]), jnp.float32)
            for tap in range(27):
                spread = spread + lax.dot_general(
                    tap_window(gpad, tap, 6, True), w_ref[tap], (((1,), (1,)), ((), ())),
                    preferred_element_type=jnp.float32,
                )
            field = jnp.concatenate([spread[0:64] + spread[64:128] + spread[128:192], spread[192:384]], axis=0)
            sig = 1.0 / (1.0 + jnp.exp(-base))
            slope = sig * (1.0 + base * (1.0 - sig))
            sendbuf[m] = (up + field * slope).astype(sendbuf.dtype)
            line_copy(sendbuf.at[m], recv.at[m], send_sem.at[m], recv_sem.at[m], here - 1, col).start()

        return carry

    lax.fori_loop(0, micro_count, step, 0)

    @pl.when(here > 0)
    def _():
        for m in range(micro_count):
            line_copy(sendbuf.at[m], recv.at[m], send_sem.at[m], recv_sem.at[m], here - 1, col).wait_send()


def backward_line(cot_local, seen, weight):
    micro_count, cells, channels = cot_local.shape
    taps = weight.shape[0]
    return pl.pallas_call(
        backward_kernel,
        out_shape=jax.ShapeDtypeStruct((taps, channels, channels), jnp.float32),
        in_specs=[pl.BlockSpec(memory_space=pltpu.VMEM)] * 3,
        out_specs=pl.BlockSpec(memory_space=pltpu.VMEM),
        scratch_shapes=[
            pltpu.VMEM(cot_local.shape, cot_local.dtype),
            pltpu.VMEM(cot_local.shape, cot_local.dtype),
            pltpu.VMEM((cells // 64 + 2, 10, 10, channels), jnp.float32),
            pltpu.VMEM((cells // 64 + 4, 10, 10, channels), jnp.float32),
            pltpu.SemaphoreType.DMA((micro_count,)),
            pltpu.SemaphoreType.DMA((micro_count,)),
        ],
        compiler_params=pltpu.CompilerParams(collective_id=3, has_side_effects=True),
    )(cot_local, seen, weight)


def per_device(clips, cotangent, weights):
    channels = weights.shape[-1]
    weight = gather_rows(weights[0]).reshape(-1, channels, channels)
    micro_count = clips.shape[0]
    clips_local = clips[:, 0].reshape(micro_count, -1, channels)
    cot_local = cotangent[:, 0].reshape(micro_count, -1, channels)
    seen, produced = forward_line(clips_local, weight)
    grad_total = backward_line(cot_local, seen, weight)
    grad_share = scatter_rows(grad_total.reshape(lax.axis_size("dp"), -1, channels))
    return (produced.reshape(clips[:, 0].shape)[None, :, None], grad_share[None])


def solution(mesh):
    placed = (
        P(None, "dp", None, None, None, None),
        P(None, "dp", None, None, None, None),
        P("section", "dp", None),
    )
    return jax.shard_map(
        per_device,
        mesh=mesh,
        in_specs=placed,
        out_specs=(P("section", None, "dp", None, None, None, None), P("section", "dp", None)),
        check_vma=False,
    )
```

time: 432 us -> 163 us (0.38)
  the two profiles are of different devices: /device:TPU:97 before, /device:TPU:6 now
where the time goes in v2:
time: 163 us; the launch traced here: 162 us
  Pallas kernels  154 us (94%)
  local copies, waits for them, and re-layouts  7.02 us (4%)
    pallas_call x1, Pallas kernels, backward_line(): pl.pallas_call(backward_kernel, out_shape=jax.ShapeDtypeStruct((taps, cha...  80.2 us
    pallas_call x1, Pallas kernels, scatter_rows(): pl.pallas_call(scatter_kernel, out_shape=jax.ShapeDtypeStruct((rows, cols...  37.8 us
    pallas_call x1, Pallas kernels, gather_rows(): pl.pallas_call(gather_kernel, out_shape=jax.ShapeDtypeStruct((peers, rows...  27.8 us
    pallas_call x1, Pallas kernels, forward_line(): pl.pallas_call(forward_kernel, out_shape=(shape, shape), in_specs=[pl.Blo...  8.39 us

profile of v2, /device:TPU:6, one launch (start us, length us, event | category | flops | bytes accessed | tf_op | source)
XLA Modules:
  0.0 161.9 jit_solution(9930149080564136123)
XLA Ops:
  0.6 27.8 %shard_map.50 = bf16[32,108,128]{2,1,0:T(8,128)(2,1)} custom-call(bf16[108,128]{1,0:T(8,128)(2,1)} %bitcast.11), custom_call_target="tpu_custom_call" | custom-call | tf_op jit(solution)/shard_map/pallas_call | solution.py:69
  28.4 2.1 %reshape.10.w_ref = bf16[27,128,128]{2,1,0:T(8,128)(2,1)} reshape(bf16[32,108,128]{2,1,0:T(8,128)(2,1)} %shard_map.50) | data formatting | bytes 1769472 | tf_op jit(solution)/shard_map/reshape | solution.py:312
  30.5 8.4 %shard_map.51 = (bf16[8,256,128]{2,1,0:T(8,128)(2,1)}, bf16[8,256,128]{2,1,0:T(8,128)(2,1)}) custom-call(bf16[8,256,128]{2,1,0:T(8,128)(2,1)} %bitcast.9, bf16[27,128,128]{2,1,0:T(8,128)(2,1)} %reshape.10.w_ref), custom_call_target="tpu_custom_call" | custom-call | tf_op jit(solution)/shard_map/pallas_call | solution.py:221
  38.9 80.2 %shard_map.52 = f32[27,128,128]{2,1,0:T(8,128)} custom-call(bf16[8,256,128]{2,1,0:T(8,128)(2,1)} %bitcast.7, bf16[8,256,128]{2,1,0:T(8,128)(2,1)} %get-tuple-element.5.seen_ref, bf16[27,128,128]{2,1,0:T(8,128)(2,1)} %reshape.10.w_ref), custom_call_target="tpu_custom_call" | custom-call | tf_op jit(solution)/shard_map/pallas_call | solution.py:293
  119.2 2.6 %reshape.11.parts_ref = f32[32,108,128]{2,1,0:T(8,128)} reshape(f32[27,128,128]{2,1,0:T(8,128)} %shard_map.52) | data formatting | bytes 3538944 | tf_op jit(solution)/shard_map/reshape | solution.py:318
  121.8 0.0 copy-start
  121.8 37.8 %shard_map.53 = f32[108,128]{1,0:T(8,128)} custom-call(f32[32,108,128]{2,1,0:T(8,128)} %reshape.11.parts_ref), custom_call_target="tpu_custom_call" | custom-call | tf_op jit(solution)/shard_map/pallas_call | solution.py:122
  159.6 1.5 copy.8
  161.1 0.0 copy-done
  161.1 0.8 copy.10
Async XLA Ops:
  121.8 39.3 %copy-start = (bf16[8,256,128]{2,1,0:T(8,128)(2,1)S(1)}, bf16[8,256,128]{2,1,0:T(8,128)(2,1)}, u32[]{:S(2)}) copy-start(bf16[8,256,128]{2,1,0:T(8,128)(2,1)} %get-tuple-element.4) | copy-start | bytes 1572868

commit v3 on v2

--- a/solution.py
+++ b/solution.py
@@ -9,58 +9,72 @@
 MESH_ID = pl.DeviceIdType.MESH
 
 
-def greet_peers(peers, here, row):
+def greet_group(here, row):
+    pair = here - here % 2
+    partner = pair + 1 - here % 2
     barrier = pltpu.get_barrier_semaphore()
+    pl.semaphore_signal(barrier, inc=1, device_id=(row, partner), device_id_type=MESH_ID)
 
     def signal(i, carry):
-        peer = lax.rem(here + i, peers)
+        peer = lax.rem(here + 2 * i, lax.axis_size("dp"))
         pl.semaphore_signal(barrier, inc=1, device_id=(row, peer), device_id_type=MESH_ID)
         return carry
 
-    lax.fori_loop(1, peers, signal, 0)
-    pl.semaphore_wait(barrier, peers - 1)
+    planes = lax.axis_size("dp") // 2
+    lax.fori_loop(1, planes, signal, 0)
+    pl.semaphore_wait(barrier, planes)
+    return partner
+
+
+def group_copy(src, dst, send_sem, recv_sem, row, peer):
+    return pltpu.make_async_remote_copy(
+        src_ref=src,
+        dst_ref=dst,
+        send_sem=send_sem,
+        recv_sem=recv_sem,
+        device_id=(row, peer),
+        device_id_type=MESH_ID,
+    )
 
 
 def gather_kernel(shard_ref, out_ref, send_sem, recv_sem):
     peers = lax.axis_size("dp")
     here = lax.axis_index("dp")
     row = lax.axis_index("section")
-    greet_peers(peers, here, row)
-
-    def outgoing(peer):
-        return pltpu.make_async_remote_copy(
-            src_ref=shard_ref,
-            dst_ref=out_ref.at[here],
-            send_sem=send_sem.at[peer],
-            recv_sem=recv_sem.at[here],
-            device_id=(row, peer),
-            device_id_type=MESH_ID,
-        )
-
-    def incoming(peer):
-        return pltpu.make_async_remote_copy(
-            src_ref=shard_ref,
-            dst_ref=out_ref.at[peer],
-            send_sem=send_sem.at[peer],
-            recv_sem=recv_sem.at[peer],
-            device_id=(row, peer),
-            device_id_type=MESH_ID,
-        )
+    partner = greet_group(here, row)
+    planes = peers // 2
+    cross = group_copy(shard_ref, out_ref.at[here], send_sem.at[here], recv_sem.at[here], row, partner)
+    cross.start()
+    out_ref[here] = shard_ref[...]
+    cross.wait_send()
+    group_copy(shard_ref, out_ref.at[partner], send_sem.at[partner], recv_sem.at[partner], row, partner).wait_recv()
+
+    def fan(i, peer):
+        own = group_copy(shard_ref, out_ref.at[here], send_sem.at[peer], recv_sem.at[here], row, peer)
+        relayed = group_copy(out_ref.at[partner], out_ref.at[partner], send_sem.at[peer + 1 - 2 * (peer % 2)],
+                             recv_sem.at[partner], row, peer)
+        return own, relayed
 
     def start(i, carry):
-        outgoing(lax.rem(here + i, peers)).start()
-        return carry
-
-    lax.fori_loop(1, peers, start, 0)
-    out_ref[here] = shard_ref[...]
+        peer = lax.rem(here + 2 * i, peers)
+        own, relayed = fan(i, peer)
+        own.start()
+        relayed.start()
+        return carry
+
+    lax.fori_loop(1, planes, start, 0)
 
     def finish(i, carry):
-        peer = lax.rem(here + i, peers)
-        outgoing(peer).wait_send()
-        incoming(peer).wait_recv()
-        return carry
-
-    lax.fori_loop(1, peers, finish, 0)
+        peer = lax.rem(here + 2 * i, peers)
+        own, relayed = fan(i, peer)
+        own.wait_send()
+        relayed.wait_send()
+        mate = peer + 1 - 2 * (peer % 2)
+        group_copy(shard_ref, out_ref.at[peer], send_sem.at[peer], recv_sem.at[peer], row, peer).wait_recv()
+        group_copy(shard_ref, out_ref.at[mate], send_sem.at[mate], recv_sem.at[mate], row, peer).wait_recv()
+        return carry
+
+    lax.fori_loop(1, planes, finish, 0)
 
 
 def gather_rows(shard):
@@ -76,45 +90,44 @@
     )(shard)
 
 
-def scatter_kernel(parts_ref, out_ref, held, send_sem, recv_sem):
+def scatter_kernel(parts_ref, out_ref, held, mine, theirs, send_sem, recv_sem, cross_sem):
     peers = lax.axis_size("dp")
     here = lax.axis_index("dp")
     row = lax.axis_index("section")
-    greet_peers(peers, here, row)
-
-    def outgoing(peer):
-        return pltpu.make_async_remote_copy(
-            src_ref=parts_ref.at[peer],
-            dst_ref=held.at[here],
-            send_sem=send_sem.at[peer],
-            recv_sem=recv_sem.at[here],
-            device_id=(row, peer),
-            device_id_type=MESH_ID,
-        )
-
-    def incoming(peer):
-        return pltpu.make_async_remote_copy(
-            src_ref=parts_ref.at[peer],
-            dst_ref=held.at[peer],
-            send_sem=send_sem.at[peer],
-            recv_sem=recv_sem.at[peer],
-            device_id=(row, peer),
-            device_id_type=MESH_ID,
-        )
+    partner = greet_group(here, row)
+    planes = peers // 2
+    slot = here // 2
+    side = here % 2
+
+    def fan(peer, block):
+        return group_copy(parts_ref.at[2 * (peer // 2) + block], held.at[slot, block],
+                          send_sem.at[peer // 2, block], recv_sem.at[slot, block], row, peer)
 
     def start(i, carry):
-        outgoing(lax.rem(here + i, peers)).start()
-        return carry
-
-    lax.fori_loop(1, peers, start, 0)
-
-    def finish(i, total):
-        peer = lax.rem(here + i, peers)
-        outgoing(peer).wait_send()
-        incoming(peer).wait_recv()
-        return total + held[peer]
-
-    out_ref[...] = lax.fori_loop(1, peers, finish, parts_ref[here])
+        peer = lax.rem(here + 2 * i, peers)
+        fan(peer, 0).start()
+        fan(peer, 1).start()
+        return carry
+
+    lax.fori_loop(1, planes, start, 0)
+
+    def finish(i, totals):
+        peer = lax.rem(here + 2 * i, peers)
+        fan(peer, 0).wait_send()
+        fan(peer, 1).wait_send()
+        source = peer // 2
+        for block in range(2):
+            group_copy(parts_ref.at[block], held.at[source, block], send_sem.at[source, block],
+                       recv_sem.at[source, block], row, peer).wait_recv()
+        return (totals[0] + held[source, 0], totals[1] + held[source, 1])
+
+    first, second = lax.fori_loop(1, planes, finish, (parts_ref[2 * slot], parts_ref[2 * slot + 1]))
+    theirs[...] = jnp.where(side == 0, second, first)
+    cross = group_copy(theirs, mine, cross_sem.at[0], cross_sem.at[1], row, partner)
+    cross.start()
+    cross.wait_send()
+    cross.wait_recv()
+    out_ref[...] = jnp.where(side == 0, first, second) + mine[...]
 
 
 def scatter_rows(parts):
@@ -125,9 +138,12 @@
         in_specs=[pl.BlockSpec(memory_space=pltpu.VMEM)],
         out_specs=pl.BlockSpec(memory_space=pltpu.VMEM),
         scratch_shapes=[
-            pltpu.VMEM((peers, rows, cols), parts.dtype),
-            pltpu.SemaphoreType.DMA((peers,)),
-            pltpu.SemaphoreType.DMA((peers,)),
+            pltpu.VMEM((peers // 2, 2, rows, cols), parts.dtype),
+            pltpu.VMEM((rows, cols), parts.dtype),
+            pltpu.VMEM((rows, cols), parts.dtype),
+            pltpu.SemaphoreType.DMA((peers // 2, 2)),
+            pltpu.SemaphoreType.DMA((peers // 2, 2)),
+            pltpu.SemaphoreType.DMA((2,)),
         ],
         compiler_params=pltpu.CompilerParams(collective_id=1, has_side_effects=True),
     )(parts)
@@ -255,12 +271,6 @@
         upstream = recv[m]
         base = seen_ref[m].astype(jnp.float32)
         squash_into(pad, base)
-        for tap in range(27):
-            wg_ref[tap] += lax.dot_general(
-                tap_window(pad, tap, 4, False), upstream, (((0,), (0,)), ((), ())),
-                preferred_element_type=jnp.float32,
-            )
-
         @pl.when(here > 0)
         def _():
             up = upstream.astype(jnp.float32)
@@ -277,6 +287,11 @@
             sendbuf[m] = (up + field * slope).astype(sendbuf.dtype)
             line_copy(sendbuf.at[m], recv.at[m], send_sem.at[m], recv_sem.at[m], here - 1, col).start()
 
+        for tap in range(27):
+            wg_ref[tap] += lax.dot_general(
+                tap_window(pad, tap, 4, False), upstream, (((0,), (0,)), ((), ())),
+                preferred_element_type=jnp.float32,
+            )
         return carry
 
     lax.fori_loop(0, micro_count, step, 0)

time: 163 us -> 130 us (0.80)
  Pallas kernels: 154 us -> 121 us
    pallas_call x1, Pallas kernels: 80.2 us -> 50.4 us  [backward_line(): pl.pallas_call(backward_kernel, out_shape=jax.ShapeDtypeStruct((taps, cha...]
    pallas_call x1, Pallas kernels: 37.8 us -> 34.7 us  [scatter_rows(): pl.pallas_call(scatter_kernel, out_shape=jax.ShapeDtypeStruct((rows, cols...]
where the time goes in v3:
time: 130 us; the launch traced here: 129 us
  Pallas kernels  121 us (93%)
  local copies, waits for them, and re-layouts  7.02 us (5%)
    pallas_call x1, Pallas kernels, backward_line(): pl.pallas_call(backward_kernel, out_shape=jax.ShapeDtypeStruct((taps, cha...  50.4 us
    pallas_call x1, Pallas kernels, scatter_rows(): pl.pallas_call(scatter_kernel, out_shape=jax.ShapeDtypeStruct((rows, cols...  34.7 us
    pallas_call x1, Pallas kernels, gather_rows(): pl.pallas_call(gather_kernel, out_shape=jax.ShapeDtypeStruct((peers, rows...  27.9 us
    pallas_call x1, Pallas kernels, forward_line(): pl.pallas_call(forward_kernel, out_shape=(shape, shape), in_specs=[pl.Blo...  8.39 us

profile of v3, /device:TPU:6, one launch (start us, length us, event | category | flops | bytes accessed | tf_op | source)
XLA Modules:
  0.0 129.1 jit_solution(8039880403867036696)
XLA Ops:
  0.6 27.9 %shard_map.50 = bf16[32,108,128]{2,1,0:T(8,128)(2,1)} custom-call(bf16[108,128]{1,0:T(8,128)(2,1)} %bitcast.11), custom_call_target="tpu_custom_call" | custom-call | tf_op jit(solution)/shard_map/pallas_call | solution.py:83
  28.6 2.1 %reshape.10.w_ref = bf16[27,128,128]{2,1,0:T(8,128)(2,1)} reshape(bf16[32,108,128]{2,1,0:T(8,128)(2,1)} %shard_map.50) | data formatting | bytes 1769472 | tf_op jit(solution)/shard_map/reshape | solution.py:327
  30.7 8.4 %shard_map.51 = (bf16[8,256,128]{2,1,0:T(8,128)(2,1)}, bf16[8,256,128]{2,1,0:T(8,128)(2,1)}) custom-call(bf16[8,256,128]{2,1,0:T(8,128)(2,1)} %bitcast.9, bf16[27,128,128]{2,1,0:T(8,128)(2,1)} %reshape.10.w_ref), custom_call_target="tpu_custom_call" | custom-call | tf_op jit(solution)/shard_map/pallas_call | solution.py:237
  39.1 50.4 %shard_map.52 = f32[27,128,128]{2,1,0:T(8,128)} custom-call(bf16[8,256,128]{2,1,0:T(8,128)(2,1)} %bitcast.7, bf16[8,256,128]{2,1,0:T(8,128)(2,1)} %get-tuple-element.5.seen_ref, bf16[27,128,128]{2,1,0:T(8,128)(2,1)} %reshape.10.w_ref), custom_call_target="tpu_custom_call" | custom-call | tf_op jit(solution)/shard_map/pallas_call | solution.py:308
  89.5 2.6 %reshape.11.parts_ref = f32[32,108,128]{2,1,0:T(8,128)} reshape(f32[27,128,128]{2,1,0:T(8,128)} %shard_map.52) | data formatting | bytes 3538944 | tf_op jit(solution)/shard_map/reshape | solution.py:333
  92.1 0.0 copy-start
  92.1 34.7 %shard_map.53 = f32[108,128]{1,0:T(8,128)} custom-call(f32[32,108,128]{2,1,0:T(8,128)} %reshape.11.parts_ref), custom_call_target="tpu_custom_call" | custom-call | tf_op jit(solution)/shard_map/pallas_call | solution.py:135
  126.8 1.5 %copy.8 = f32[1,108,128]{2,0,1:T(1,128)} copy(f32[1,108,128]{2,1,0:T(8,128)} %bitcast.10) | data formatting | bytes 110592
  128.3 0.0 copy-done
  128.3 0.8 copy.10
Async XLA Ops:
  92.1 36.2 %copy-start = (bf16[8,256,128]{2,1,0:T(8,128)(2,1)S(1)}, bf16[8,256,128]{2,1,0:T(8,128)(2,1)}, u32[]{:S(2)}) copy-start(bf16[8,256,128]{2,1,0:T(8,128)(2,1)} %get-tuple-element.4) | copy-start | bytes 1572868

commit v4 on v3

--- a/solution.py
+++ b/solution.py
@@ -45,9 +45,6 @@
     planes = peers // 2
     cross = group_copy(shard_ref, out_ref.at[here], send_sem.at[here], recv_sem.at[here], row, partner)
     cross.start()
-    out_ref[here] = shard_ref[...]
-    cross.wait_send()
-    group_copy(shard_ref, out_ref.at[partner], send_sem.at[partner], recv_sem.at[partner], row, partner).wait_recv()
 
     def fan(i, peer):
         own = group_copy(shard_ref, out_ref.at[here], send_sem.at[peer], recv_sem.at[here], row, peer)
@@ -55,14 +52,19 @@
                              recv_sem.at[partner], row, peer)
         return own, relayed
 
-    def start(i, carry):
-        peer = lax.rem(here + 2 * i, peers)
-        own, relayed = fan(i, peer)
-        own.start()
-        relayed.start()
-        return carry
-
-    lax.fori_loop(1, planes, start, 0)
+    def start_own(i, carry):
+        fan(i, lax.rem(here + 2 * i, peers))[0].start()
+        return carry
+
+    def start_relay(i, carry):
+        fan(i, lax.rem(here + 2 * i, peers))[1].start()
+        return carry
+
+    lax.fori_loop(1, planes, start_own, 0)
+    out_ref[here] = shard_ref[...]
+    cross.wait_send()
+    group_copy(shard_ref, out_ref.at[partner], send_sem.at[partner], recv_sem.at[partner], row, partner).wait_recv()
+    lax.fori_loop(1, planes, start_relay, 0)
 
     def finish(i, carry):
         peer = lax.rem(here + 2 * i, peers)
@@ -119,9 +121,10 @@
         for block in range(2):
             group_copy(parts_ref.at[block], held.at[source, block], send_sem.at[source, block],
                        recv_sem.at[source, block], row, peer).wait_recv()
-        return (totals[0] + held[source, 0], totals[1] + held[source, 1])
-
-    first, second = lax.fori_loop(1, planes, finish, (parts_ref[2 * slot], parts_ref[2 * slot + 1]))
+        return (totals[0] + held[source, 0].astype(jnp.float32), totals[1] + held[source, 1].astype(jnp.float32))
+
+    start_totals = (parts_ref[2 * slot].astype(jnp.float32), parts_ref[2 * slot + 1].astype(jnp.float32))
+    first, second = lax.fori_loop(1, planes, finish, start_totals)
     theirs[...] = jnp.where(side == 0, second, first)
     cross = group_copy(theirs, mine, cross_sem.at[0], cross_sem.at[1], row, partner)
     cross.start()
@@ -134,13 +137,13 @@
     peers, rows, cols = parts.shape
     return pl.pallas_call(
         scatter_kernel,
-        out_shape=jax.ShapeDtypeStruct((rows, cols), parts.dtype),
+        out_shape=jax.ShapeDtypeStruct((rows, cols), jnp.float32),
         in_specs=[pl.BlockSpec(memory_space=pltpu.VMEM)],
         out_specs=pl.BlockSpec(memory_space=pltpu.VMEM),
         scratch_shapes=[
             pltpu.VMEM((peers // 2, 2, rows, cols), parts.dtype),
-            pltpu.VMEM((rows, cols), parts.dtype),
-            pltpu.VMEM((rows, cols), parts.dtype),
+            pltpu.VMEM((rows, cols), jnp.float32),
+            pltpu.VMEM((rows, cols), jnp.float32),
             pltpu.SemaphoreType.DMA((peers // 2, 2)),
             pltpu.SemaphoreType.DMA((peers // 2, 2)),
             pltpu.SemaphoreType.DMA((2,)),
@@ -330,7 +333,7 @@
     cot_local = cotangent[:, 0].reshape(micro_count, -1, channels)
     seen, produced = forward_line(clips_local, weight)
     grad_total = backward_line(cot_local, seen, weight)
-    grad_share = scatter_rows(grad_total.reshape(lax.axis_size("dp"), -1, channels))
+    grad_share = scatter_rows(grad_total.astype(jnp.bfloat16).reshape(lax.axis_size("dp"), -1, channels))
     return (produced.reshape(clips[:, 0].shape)[None, :, None], grad_share[None])
 
 

time: 130 us -> 115 us (0.88)
  Pallas kernels: 121 us -> 106 us
  other arithmetic: 0 us -> 1.63 us
  local copies, waits for them, and re-layouts: 7.02 us -> 5.45 us
    pallas_call x1, Pallas kernels: 34.7 us -> 24.6 us  [scatter_rows(): pl.pallas_call(scatter_kernel, out_shape=jax.ShapeDtypeStruct((rows, cols...]
    pallas_call x1, Pallas kernels: 27.9 us -> 23.1 us  [gather_rows(): pl.pallas_call(gather_kernel, out_shape=jax.ShapeDtypeStruct((peers, rows...]
    convert_element_type x0 -> x1, other arithmetic: none -> 1.63 us  [per_device(): grad_total.astype(jnp.bfloat16).reshape(lax.axis_size('dp'), -1, channels)]
    reshape x1, local copies, waits for them, and re-layouts: 2.6 us -> 1.07 us  [per_device(): grad_total.astype(jnp.bfloat16).reshape(lax.axis_size('dp'), -1, channels)]
where the time goes in v4:
time: 115 us; the launch traced here: 114 us
  Pallas kernels  106 us (92%)
  local copies, waits for them, and re-layouts  5.45 us (5%)
  other arithmetic  1.63 us (1%)
    pallas_call x1, Pallas kernels, backward_line(): pl.pallas_call(backward_kernel, out_shape=jax.ShapeDtypeStruct((taps, cha...  50.4 us
    pallas_call x1, Pallas kernels, scatter_rows(): pl.pallas_call(scatter_kernel, out_shape=jax.ShapeDtypeStruct((rows, cols...  24.6 us
    pallas_call x1, Pallas kernels, gather_rows(): pl.pallas_call(gather_kernel, out_shape=jax.ShapeDtypeStruct((peers, rows...  23.1 us
    pallas_call x1, Pallas kernels, forward_line(): pl.pallas_call(forward_kernel, out_shape=(shape, shape), in_specs=[pl.Blo...  8.41 us

profile of v4, /device:TPU:6, one launch (start us, length us, event | category | flops | bytes accessed | tf_op | source)
XLA Modules:
  0.0 114.3 jit_solution(14236097805232433548)
XLA Ops:
  0.6 23.1 %shard_map.50 = bf16[32,108,128]{2,1,0:T(8,128)(2,1)} custom-call(bf16[108,128]{1,0:T(8,128)(2,1)} %bitcast.11), custom_call_target="tpu_custom_call" | custom-call | tf_op jit(solution)/shard_map/pallas_call | solution.py:85
  23.7 2.1 %reshape.10.w_ref = bf16[27,128,128]{2,1,0:T(8,128)(2,1)} reshape(bf16[32,108,128]{2,1,0:T(8,128)(2,1)} %shard_map.50) | data formatting | bytes 1769472 | tf_op jit(solution)/shard_map/reshape | solution.py:330
  25.8 8.4 %shard_map.51 = (bf16[8,256,128]{2,1,0:T(8,128)(2,1)}, bf16[8,256,128]{2,1,0:T(8,128)(2,1)}) custom-call(bf16[8,256,128]{2,1,0:T(8,128)(2,1)} %bitcast.9, bf16[27,128,128]{2,1,0:T(8,128)(2,1)} %reshape.10.w_ref), custom_call_target="tpu_custom_call" | custom-call | tf_op jit(solution)/shard_map/pallas_call | solution.py:240
  34.2 50.4 %shard_map.52 = f32[27,128,128]{2,1,0:T(8,128)} custom-call(bf16[8,256,128]{2,1,0:T(8,128)(2,1)} %bitcast.7, bf16[8,256,128]{2,1,0:T(8,128)(2,1)} %get-tuple-element.5.seen_ref, bf16[27,128,128]{2,1,0:T(8,128)(2,1)} %reshape.10.w_ref), custom_call_target="tpu_custom_call" | custom-call | tf_op jit(solution)/shard_map/pallas_call | solution.py:311
  84.6 1.6 %convert_element_type.3 = bf16[27,128,128]{2,1,0:T(8,128)(2,1)S(1)} convert(f32[27,128,128]{2,1,0:T(8,128)} %shard_map.52) | non-fusion elementwise | flops 442368 | bytes 2654208 | tf_op jit(solution)/shard_map/convert_element_type | solution.py:336
  86.3 0.0 copy-start
  86.3 1.1 reshape.11.parts_ref
  87.4 24.6 %shard_map.53 = f32[108,128]{1,0:T(8,128)} custom-call(bf16[32,108,128]{2,1,0:T(8,128)(2,1)} %reshape.11.parts_ref), custom_call_target="tpu_custom_call" | custom-call | tf_op jit(solution)/shard_map/pallas_call | solution.py:138
  112.0 1.5 %copy.8 = f32[1,108,128]{2,0,1:T(1,128)} copy(f32[1,108,128]{2,1,0:T(8,128)} %bitcast.10) | data formatting | bytes 110592
  113.5 0.0 copy-done
  113.5 0.8 copy.10
Async XLA Ops:
  86.3 27.2 %copy-start = (bf16[8,256,128]{2,1,0:T(8,128)(2,1)S(1)}, bf16[8,256,128]{2,1,0:T(8,128)(2,1)}, u32[]{:S(2)}) copy-start(bf16[8,256,128]{2,1,0:T(8,128)(2,1)} %get-tuple-element.4) | copy-start | bytes 1572868

commit v5 on v4

--- a/solution.py
+++ b/solution.py
@@ -280,21 +280,16 @@
             gpad[2:6, 1:9, 1:9, :] = up.reshape(4, 8, 8, up.shape[-1])
             spread = jnp.zeros((384, up.shape[-1]), jnp.float32)
             for tap in range(27):
-                spread = spread + lax.dot_general(
-                    tap_window(gpad, tap, 6, True), w_ref[tap], (((1,), (1,)), ((), ())),
-                    preferred_element_type=jnp.float32,
-                )
+                spread = spread + jnp.dot(tap_window(gpad, tap, 6, True), w_ref[tap], preferred_element_type=jnp.float32)
             field = jnp.concatenate([spread[0:64] + spread[64:128] + spread[128:192], spread[192:384]], axis=0)
             sig = 1.0 / (1.0 + jnp.exp(-base))
             slope = sig * (1.0 + base * (1.0 - sig))
             sendbuf[m] = (up + field * slope).astype(sendbuf.dtype)
             line_copy(sendbuf.at[m], recv.at[m], send_sem.at[m], recv_sem.at[m], here - 1, col).start()
 
+        upstream_t = upstream.T
         for tap in range(27):
-            wg_ref[tap] += lax.dot_general(
-                tap_window(pad, tap, 4, False), upstream, (((0,), (0,)), ((), ())),
-                preferred_element_type=jnp.float32,
-            )
+            wg_ref[tap] += jnp.dot(upstream_t, tap_window(pad, tap, 4, False), preferred_element_type=jnp.float32)
         return carry
 
     lax.fori_loop(0, micro_count, step, 0)
@@ -332,8 +327,9 @@
     clips_local = clips[:, 0].reshape(micro_count, -1, channels)
     cot_local = cotangent[:, 0].reshape(micro_count, -1, channels)
     seen, produced = forward_line(clips_local, weight)
-    grad_total = backward_line(cot_local, seen, weight)
-    grad_share = scatter_rows(grad_total.astype(jnp.bfloat16).reshape(lax.axis_size("dp"), -1, channels))
+    grad_t = backward_line(cot_local, seen, jnp.swapaxes(weight, 1, 2))
+    grad_total = jnp.swapaxes(grad_t, 1, 2).astype(jnp.bfloat16)
+    grad_share = scatter_rows(grad_total.reshape(lax.axis_size("dp"), -1, channels))
     return (produced.reshape(clips[:, 0].shape)[None, :, None], grad_share[None])
 
 

time: 115 us -> 117 us (1.017)
  local copies, waits for them, and re-layouts: 5.45 us -> 7.59 us
    convert_element_type x0 -> x1, local copies, waits for them, and re-layouts: none -> 1.32 us  [per_device(): grad_total = jnp.swapaxes(grad_t, 1, 2).astype(jnp.bfloat16)]
    reshape x1 -> x2, local copies, waits for them, and re-layouts: 2.08 us -> 2.9 us  [per_device(): weight = gather_rows(weights[0]).reshape(-1, channels, channels)]
where the time goes in v5:
time: 117 us; the launch traced here: 116 us
  Pallas kernels  106 us (91%)
  local copies, waits for them, and re-layouts  7.59 us (6%)
  other arithmetic  1.63 us (1%)
    pallas_call x1, Pallas kernels, backward_line(): pl.pallas_call(backward_kernel, out_shape=jax.ShapeDtypeStruct((taps, cha...  50.2 us
    pallas_call x1, Pallas kernels, scatter_rows(): pl.pallas_call(scatter_kernel, out_shape=jax.ShapeDtypeStruct((rows, cols...  24.6 us
    pallas_call x1, Pallas kernels, gather_rows(): pl.pallas_call(gather_kernel, out_shape=jax.ShapeDtypeStruct((peers, rows...  23.1 us
    pallas_call x1, Pallas kernels, forward_line(): pl.pallas_call(forward_kernel, out_shape=(shape, shape), in_specs=[pl.Blo...  8.41 us
    reshape x2, local copies, waits for them, and re-layouts, per_device(): weight = gather_rows(weights[0]).reshape(-1, channels, channels)  2.9 us

profile of v5, /device:TPU:6, one launch (start us, length us, event | category | flops | bytes accessed | tf_op | source)
XLA Modules:
  0.0 116.2 jit_solution(14922538024248529215)
XLA Ops:
  0.6 23.1 %shard_map.50 = bf16[32,108,128]{2,1,0:T(8,128)(2,1)} custom-call(bf16[108,128]{1,0:T(8,128)(2,1)} %bitcast.15), custom_call_target="tpu_custom_call" | custom-call | tf_op jit(solution)/shard_map/pallas_call | solution.py:85
  23.7 1.3 %reshape.10.w_ref = bf16[27,128,128]{2,1,0:T(8,128)(2,1)S(1)} reshape(bf16[32,108,128]{2,1,0:T(8,128)(2,1)} %shard_map.50) | data formatting | bytes 1769472 | tf_op jit(solution)/shard_map/reshape | solution.py:325
  25.0 0.0 copy-start
  25.0 1.6 %copy.9 = bf16[27,128,128]{1,2,0:T(8,128)(2,1)} copy(bf16[27,128,128]{2,1,0:T(8,128)(2,1)S(1)} %reshape.10.w_ref) | data formatting | bytes 1769472 | tf_op jit(solution)/shard_map/reshape | solution.py:325
  26.6 0.0 copy-done
  26.6 8.4 %shard_map.51 = (bf16[8,256,128]{2,1,0:T(8,128)(2,1)}, bf16[8,256,128]{2,1,0:T(8,128)(2,1)}) custom-call(bf16[8,256,128]{2,1,0:T(8,128)(2,1)} %bitcast.13, bf16[27,128,128]{2,1,0:T(8,128)(2,1)} %copy-done), custom_call_target="tpu_custom_call" | custom-call | tf_op jit(solution)/shard_map/pallas_call | solution.py:240
  35.1 50.2 %shard_map.52 = f32[27,128,128]{2,1,0:T(8,128)} custom-call(bf16[8,256,128]{2,1,0:T(8,128)(2,1)} %bitcast.11, bf16[8,256,128]{2,1,0:T(8,128)(2,1)} %get-tuple-element.5.seen_ref, bf16[27,128,128]{2,1,0:T(8,128)(2,1)} %bitcast.10), custom_call_target="tpu_custom_call" | custom-call | tf_op jit(solution)/shard_map/pallas_call | solution.py:306
  85.2 1.6 %convert_bitcast_fusion = bf16[27,128,128]{1,2,0:T(8,128)(2,1)S(1)} fusion(f32[27,128,128]{2,1,0:T(8,128)} %shard_map.52), kind=kLoop, calls=%fused_computation | loop fusion | flops 442368 | bytes 2654208 | tf_op jit(solution)/shard_map/convert_element_type | solution.py:331
  86.9 1.3 %copy.10 = bf16[27,128,128]{2,1,0:T(8,128)(2,1)S(1)} copy(bf16[27,128,128]{1,2,0:T(8,128)(2,1)S(1)} %convert_bitcast_fusion) | data formatting | bytes 1769472 | tf_op jit(solution)/shard_map/convert_element_type | solution.py:331
  88.2 0.0 copy-start.1
  88.2 1.1 reshape.11.parts_ref
  89.3 24.6 %shard_map.53 = f32[108,128]{1,0:T(8,128)} custom-call(bf16[32,108,128]{2,1,0:T(8,128)(2,1)} %reshape.11.parts_ref), custom_call_target="tpu_custom_call" | custom-call | tf_op jit(solution)/shard_map/pallas_call | solution.py:138
  113.9 1.5 %copy.12 = f32[1,108,128]{2,0,1:T(1,128)} copy(f32[1,108,128]{2,1,0:T(8,128)} %bitcast.14) | data formatting | bytes 110592
  115.4 0.0 copy-done.1
  115.4 0.8 copy.14
Async XLA Ops:
  25.0 1.6 %copy-start = (bf16[27,128,128]{2,1,0:T(8,128)(2,1)}, bf16[27,128,128]{2,1,0:T(8,128)(2,1)S(1)}, u32[]{:S(2)}) copy-start(bf16[27,128,128]{2,1,0:T(8,128)(2,1)S(1)} %reshape.10.w_ref) | copy-start | bytes 2654212
  88.2 27.2 %copy-start.1 = (bf16[8,256,128]{2,1,0:T(8,128)(2,1)S(1)}, bf16[8,256,128]{2,1,0:T(8,128)(2,1)}, u32[]{:S(2)}) copy-start(bf16[8,256,128]{2,1,0:T(8,128)(2,1)} %get-tuple-element.4) | copy-start | bytes 1572868

commit v6 on v5

--- a/solution.py
+++ b/solution.py
@@ -159,14 +159,18 @@
     pad_ref[0:2, 1:9, 1:9, :] = jnp.broadcast_to(field[0:1], (2,) + field.shape[1:])
 
 
-def tap_window(pad_ref, tap, frames, base):
-    offset_time, offset_row, offset_col = tap // 9, (tap // 3) % 3, tap % 3
-    if base:
-        t0, r0, c0 = 2 - offset_time, 2 - offset_row, 2 - offset_col
-    else:
-        t0, r0, c0 = offset_time, offset_row, offset_col
-    window = pad_ref[t0 : t0 + frames, r0 : r0 + 8, c0 : c0 + 8, :]
-    return window.reshape(frames * 64, window.shape[-1]).astype(jnp.bfloat16)
+def fill_columns(pad_ref, cols_ref, frames, flipped):
+    channels = pad_ref.shape[-1]
+    for c0 in range(3):
+        shifted = pad_ref[:, :, c0 : c0 + 8, :]
+        offset_col = 2 - c0 if flipped else c0
+        for offset_time in range(3):
+            for offset_row in range(3):
+                t0 = 2 - offset_time if flipped else offset_time
+                r0 = 2 - offset_row if flipped else offset_row
+                tap = offset_time * 9 + offset_row * 3 + offset_col
+                window = shifted[t0 : t0 + frames, r0 : r0 + 8].reshape(frames * 64, channels)
+                cols_ref[:, tap * channels : (tap + 1) * channels] = window.astype(cols_ref.dtype)
 
 
 def greet_line(here, count, col):
@@ -195,7 +199,7 @@
     )
 
 
-def forward_kernel(clips_ref, w_ref, seen_ref, out_ref, recv, pad, send_sem, recv_sem):
+def forward_kernel(clips_ref, w_ref, seen_ref, out_ref, recv, pad, cols, send_sem, recv_sem):
     count = lax.axis_size("section")
     here = lax.axis_index("section")
     col = lax.axis_index("dp")
@@ -215,9 +219,8 @@
 
         base = seen_ref[m].astype(jnp.float32)
         squash_into(pad, base)
-        total = base
-        for tap in range(27):
-            total = total + jnp.dot(tap_window(pad, tap, 4, False), w_ref[tap], preferred_element_type=jnp.float32)
+        fill_columns(pad, cols, 4, False)
+        total = base + jnp.dot(cols[...], w_ref[...], preferred_element_type=jnp.float32)
         out_ref[m] = total.astype(out_ref.dtype)
 
         @pl.when(here < count - 1)
@@ -245,6 +248,7 @@
         scratch_shapes=[
             pltpu.VMEM(clips_local.shape, clips_local.dtype),
             pltpu.VMEM((cells // 64 + 2, 10, 10, channels), jnp.float32),
+            pltpu.VMEM((cells, weight.shape[0]), jnp.bfloat16),
             pltpu.SemaphoreType.DMA((micro_count,)),
             pltpu.SemaphoreType.DMA((micro_count,)),
         ],
@@ -252,7 +256,7 @@
     )(clips_local, weight)
 
 
-def backward_kernel(cot_ref, seen_ref, w_ref, wg_ref, recv, sendbuf, pad, gpad, send_sem, recv_sem):
+def backward_kernel(cot_ref, seen_ref, w_ref, wg_ref, recv, sendbuf, pad, gpad, cols, gcols, send_sem, recv_sem):
     count = lax.axis_size("section")
     here = lax.axis_index("section")
     col = lax.axis_index("dp")
@@ -278,18 +282,16 @@
         def _():
             up = upstream.astype(jnp.float32)
             gpad[2:6, 1:9, 1:9, :] = up.reshape(4, 8, 8, up.shape[-1])
-            spread = jnp.zeros((384, up.shape[-1]), jnp.float32)
-            for tap in range(27):
-                spread = spread + jnp.dot(tap_window(gpad, tap, 6, True), w_ref[tap], preferred_element_type=jnp.float32)
+            fill_columns(gpad, gcols, 6, True)
+            spread = jnp.dot(gcols[...], w_ref[...], preferred_element_type=jnp.float32)
             field = jnp.concatenate([spread[0:64] + spread[64:128] + spread[128:192], spread[192:384]], axis=0)
             sig = 1.0 / (1.0 + jnp.exp(-base))
             slope = sig * (1.0 + base * (1.0 - sig))
             sendbuf[m] = (up + field * slope).astype(sendbuf.dtype)
             line_copy(sendbuf.at[m], recv.at[m], send_sem.at[m], recv_sem.at[m], here - 1, col).start()
 
-        upstream_t = upstream.T
-        for tap in range(27):
-            wg_ref[tap] += jnp.dot(upstream_t, tap_window(pad, tap, 4, False), preferred_element_type=jnp.float32)
+        fill_columns(pad, cols, 4, False)
+        wg_ref[...] += jnp.dot(upstream.T, cols[...], preferred_element_type=jnp.float32)
         return carry
 
     lax.fori_loop(0, micro_count, step, 0)
@@ -302,10 +304,10 @@
 
 def backward_line(cot_local, seen, weight):
     micro_count, cells, channels = cot_local.shape
-    taps = weight.shape[0]
+    rows = weight.shape[0]
     return pl.pallas_call(
         backward_kernel,
-        out_shape=jax.ShapeDtypeStruct((taps, channels, channels), jnp.float32),
+        out_shape=jax.ShapeDtypeStruct((channels, rows), jnp.float32),
         in_specs=[pl.BlockSpec(memory_space=pltpu.VMEM)] * 3,
         out_specs=pl.BlockSpec(memory_space=pltpu.VMEM),
         scratch_shapes=[
@@ -313,6 +315,8 @@
             pltpu.VMEM(cot_local.shape, cot_local.dtype),
             pltpu.VMEM((cells // 64 + 2, 10, 10, channels), jnp.float32),
             pltpu.VMEM((cells // 64 + 4, 10, 10, channels), jnp.float32),
+            pltpu.VMEM((cells, rows), jnp.bfloat16),
+            pltpu.VMEM((cells * 3 // 2, rows), jnp.bfloat16),
             pltpu.SemaphoreType.DMA((micro_count,)),
             pltpu.SemaphoreType.DMA((micro_count,)),
         ],
@@ -322,13 +326,15 @@
 
 def per_device(clips, cotangent, weights):
     channels = weights.shape[-1]
-    weight = gather_rows(weights[0]).reshape(-1, channels, channels)
+    weight = gather_rows(weights[0]).reshape(-1, channels)
+    taps = weight.shape[0] // channels
     micro_count = clips.shape[0]
     clips_local = clips[:, 0].reshape(micro_count, -1, channels)
     cot_local = cotangent[:, 0].reshape(micro_count, -1, channels)
     seen, produced = forward_line(clips_local, weight)
-    grad_t = backward_line(cot_local, seen, jnp.swapaxes(weight, 1, 2))
-    grad_total = jnp.swapaxes(grad_t, 1, 2).astype(jnp.bfloat16)
+    weight_t = jnp.swapaxes(weight.reshape(taps, channels, channels), 1, 2).reshape(-1, channels)
+    grad_t = backward_line(cot_local, seen, weight_t)
+    grad_total = grad_t.T.astype(jnp.bfloat16)
     grad_share = scatter_rows(grad_total.reshape(lax.axis_size("dp"), -1, channels))
     return (produced.reshape(clips[:, 0].shape)[None, :, None], grad_share[None])
 

time: 117 us -> 125 us (1.068)
  local copies, waits for them, and re-layouts: 7.59 us -> 12.4 us
  Pallas kernels: 106 us -> 110 us
    reshape x1 -> x2, local copies, waits for them, and re-layouts: 1.07 us -> 5.97 us  [per_device(): grad_total.reshape(lax.axis_size('dp'), -1, channels)]
    pallas_call x1, Pallas kernels: 50.2 us -> 52.6 us  [backward_line(): pl.pallas_call(backward_kernel, out_shape=jax.ShapeDtypeStruct((channels,...]
    reshape x2 -> x1, local copies, waits for them, and re-layouts: 2.9 us -> 1.07 us  [per_device(): weight = gather_rows(weights[0]).reshape(-1, channels)]
    transpose x0 -> x1, local copies, waits for them, and re-layouts: none -> 1.62 us  [per_device(): jnp.swapaxes(weight.reshape(taps, channels, channels), 1, 2)]
    another operation x0 -> x1, local copies, waits for them, and re-layouts: none -> 1.35 us  [per_device(): weight.reshape(taps, channels, channels)]
    convert_element_type x1 -> x0, local copies, waits for them, and re-layouts: 1.32 us -> none  [per_device(): grad_total = jnp.swapaxes(grad_t, 1, 2).astype(jnp.bfloat16)]
where the time goes in v6:
time: 125 us
  Pallas kernels  110 us (88%)
  local copies, waits for them, and re-layouts  12.4 us (10%)
  other arithmetic  1.57 us (1%)
    pallas_call x1, Pallas kernels, backward_line(): pl.pallas_call(backward_kernel, out_shape=jax.ShapeDtypeStruct((channels,...  52.6 us
    pallas_call x1, Pallas kernels, scatter_rows(): pl.pallas_call(scatter_kernel, out_shape=jax.ShapeDtypeStruct((rows, cols...  24.7 us
    pallas_call x1, Pallas kernels, gather_rows(): pl.pallas_call(gather_kernel, out_shape=jax.ShapeDtypeStruct((peers, rows...  23.1 us
    pallas_call x1, Pallas kernels, forward_line(): pl.pallas_call(forward_kernel, out_shape=(shape, shape), in_specs=[pl.Blo...  9.56 us
    reshape x2, local copies, waits for them, and re-layouts, per_device(): grad_total.reshape(lax.axis_size('dp'), -1, channels)  5.97 us

profile of v6, /device:TPU:6, one launch (start us, length us, event | category | flops | bytes accessed | tf_op | source)
XLA Modules:
  0.0 124.6 jit_solution(7647025697244421675)
XLA Ops:
  0.6 23.1 %shard_map.50 = bf16[32,108,128]{2,1,0:T(8,128)(2,1)} custom-call(bf16[108,128]{1,0:T(8,128)(2,1)} %bitcast.19), custom_call_target="tpu_custom_call" | custom-call | tf_op jit(solution)/shard_map/pallas_call | solution.py:85
  23.7 0.0 copy-start
  23.7 1.3 %reshape_reshape.3 = bf16[27,128,128]{2,1,0:T(8,128)(2,1)S(1)} reshape(bf16[32,108,128]{2,1,0:T(8,128)(2,1)} %shard_map.50) | data formatting | bytes 1769472 | tf_op jit(solution)/shard_map/reshape;reshape | solution.py:335
  25.1 0.1 copy-done
  25.2 1.1 reshape.13.w_ref
  26.2 1.6 %copy.9 = bf16[27,128,128]{2,1,0:T(8,128)(2,1)} copy(bf16[27,128,128]{1,2,0:T(8,128)(2,1)S(1)} %bitcast.14) | data formatting | bytes 1769472 | tf_op jit(solution)/shard_map/transpose | solution.py:335
  27.9 9.6 %shard_map.51 = (bf16[8,256,128]{2,1,0:T(8,128)(2,1)}, bf16[8,256,128]{2,1,0:T(8,128)(2,1)}) custom-call(bf16[8,256,128]{2,1,0:T(8,128)(2,1)} %bitcast.17, bf16[3456,128]{1,0:T(8,128)(2,1)} %reshape.13.w_ref), custom_call_target="tpu_custom_call" | custom-call | tf_op jit(solution)/shard_map/pallas_call | solution.py:243
  37.4 52.6 %shard_map.52 = f32[128,3456]{1,0:T(8,128)} custom-call(bf16[8,256,128]{2,1,0:T(8,128)(2,1)} %bitcast.15, bf16[8,256,128]{2,1,0:T(8,128)(2,1)} %get-tuple-element.5.seen_ref, bf16[3456,128]{1,0:T(8,128)(2,1)} %bitcast.13), custom_call_target="tpu_custom_call" | custom-call | tf_op jit(solution)/shard_map/pallas_call | solution.py:308
  90.0 1.6 %convert_bitcast_fusion = bf16[3456,128]{0,1:T(8,128)(2,1)S(1)} fusion(f32[128,3456]{1,0:T(8,128)} %shard_map.52), kind=kLoop, calls=%fused_computation | loop fusion | flops 442368 | bytes 2654208 | tf_op jit(solution)/shard_map/convert_element_type | solution.py:337
  91.6 4.2 %reshape.16 = bf16[32,108,128]{1,0,2:T(8,128)(2,1)S(1)} reshape(bf16[3456,128]{0,1:T(8,128)(2,1)S(1)} %convert_bitcast_fusion) | data formatting | bytes 1769472 | tf_op jit(solution)/shard_map/reshape | solution.py:338
  95.8 0.0 copy-start.1
  95.8 1.8 %copy.13.parts_ref = bf16[32,108,128]{2,1,0:T(8,128)(2,1)} copy(bf16[32,108,128]{1,0,2:T(8,128)(2,1)S(1)} %reshape.16) | data formatting | bytes 1769472 | tf_op jit(solution)/shard_map/reshape | solution.py:338
  97.6 24.7 %shard_map.53 = f32[108,128]{1,0:T(8,128)} custom-call(bf16[32,108,128]{2,1,0:T(8,128)(2,1)} %copy.13.parts_ref), custom_call_target="tpu_custom_call" | custom-call | tf_op jit(solution)/shard_map/pallas_call | solution.py:138
  122.3 1.5 %copy.12 = f32[1,108,128]{2,0,1:T(1,128)} copy(f32[1,108,128]{2,1,0:T(8,128)} %bitcast.18) | data formatting | bytes 110592
  123.8 0.0 copy-done.1
  123.8 0.8 copy.15
Async XLA Ops:
  23.7 1.5 %copy-start = (bf16[32,108,128]{2,1,0:T(8,128)(2,1)S(1)}, bf16[32,108,128]{2,1,0:T(8,128)(2,1)}, u32[]{:S(2)}) copy-start(bf16[32,108,128]{2,1,0:T(8,128)(2,1)} %shard_map.50) | copy-start | bytes 2654212
  95.8 28.0 %copy-start.1 = (bf16[8,256,128]{2,1,0:T(8,128)(2,1)S(1)}, bf16[8,256,128]{2,1,0:T(8,128)(2,1)}, u32[]{:S(2)}) copy-start(bf16[8,256,128]{2,1,0:T(8,128)(2,1)} %get-tuple-element.4) | copy-start | bytes 1572868

commit v7 on v4

--- a/solution.py
+++ b/solution.py
@@ -159,14 +159,17 @@
     pad_ref[0:2, 1:9, 1:9, :] = jnp.broadcast_to(field[0:1], (2,) + field.shape[1:])
 
 
-def tap_window(pad_ref, tap, frames, base):
-    offset_time, offset_row, offset_col = tap // 9, (tap // 3) % 3, tap % 3
-    if base:
-        t0, r0, c0 = 2 - offset_time, 2 - offset_row, 2 - offset_col
-    else:
-        t0, r0, c0 = offset_time, offset_row, offset_col
-    window = pad_ref[t0 : t0 + frames, r0 : r0 + 8, c0 : c0 + 8, :]
-    return window.reshape(frames * 64, window.shape[-1]).astype(jnp.bfloat16)
+def tap_windows(pad_ref, frames, flipped):
+    channels = pad_ref.shape[-1]
+    for c0 in range(3):
+        shifted = pad_ref[:, :, c0 : c0 + 8, :]
+        offset_col = 2 - c0 if flipped else c0
+        for offset_time in range(3):
+            for offset_row in range(3):
+                t0 = 2 - offset_time if flipped else offset_time
+                r0 = 2 - offset_row if flipped else offset_row
+                window = shifted[t0 : t0 + frames, r0 : r0 + 8].reshape(frames * 64, channels)
+                yield offset_time * 9 + offset_row * 3 + offset_col, window.astype(jnp.bfloat16)
 
 
 def greet_line(here, count, col):
@@ -216,8 +219,8 @@
         base = seen_ref[m].astype(jnp.float32)
         squash_into(pad, base)
         total = base
-        for tap in range(27):
-            total = total + jnp.dot(tap_window(pad, tap, 4, False), w_ref[tap], preferred_element_type=jnp.float32)
+        for tap, window in tap_windows(pad, 4, False):
+            total = total + jnp.dot(window, w_ref[tap], preferred_element_type=jnp.float32)
         out_ref[m] = total.astype(out_ref.dtype)
 
         @pl.when(here < count - 1)
@@ -279,9 +282,9 @@
             up = upstream.astype(jnp.float32)
             gpad[2:6, 1:9, 1:9, :] = up.reshape(4, 8, 8, up.shape[-1])
             spread = jnp.zeros((384, up.shape[-1]), jnp.float32)
-            for tap in range(27):
+            for tap, window in tap_windows(gpad, 6, True):
                 spread = spread + lax.dot_general(
-                    tap_window(gpad, tap, 6, True), w_ref[tap], (((1,), (1,)), ((), ())),
+                    window, w_ref[tap], (((1,), (1,)), ((), ())),
                     preferred_element_type=jnp.float32,
                 )
             field = jnp.concatenate([spread[0:64] + spread[64:128] + spread[128:192], spread[192:384]], axis=0)
@@ -290,9 +293,9 @@
             sendbuf[m] = (up + field * slope).astype(sendbuf.dtype)
             line_copy(sendbuf.at[m], recv.at[m], send_sem.at[m], recv_sem.at[m], here - 1, col).start()
 
-        for tap in range(27):
+        for tap, window in tap_windows(pad, 4, False):
             wg_ref[tap] += lax.dot_general(
-                tap_window(pad, tap, 4, False), upstream, (((0,), (0,)), ((), ())),
+                window, upstream, (((0,), (0,)), ((), ())),
                 preferred_element_type=jnp.float32,
             )
         return carry

time: 115 us -> 115 us (level)
  no operation moved by 1% of the time
where the time goes in v7:
time: 115 us; the launch traced here: 114 us
  Pallas kernels  107 us (93%)
  local copies, waits for them, and re-layouts  5.45 us (5%)
  other arithmetic  1.63 us (1%)
    pallas_call x1, Pallas kernels, backward_line(): pl.pallas_call(backward_kernel, out_shape=jax.ShapeDtypeStruct((taps, cha...  50.6 us
    pallas_call x1, Pallas kernels, scatter_rows(): pl.pallas_call(scatter_kernel, out_shape=jax.ShapeDtypeStruct((rows, cols...  24.6 us
    pallas_call x1, Pallas kernels, gather_rows(): pl.pallas_call(gather_kernel, out_shape=jax.ShapeDtypeStruct((peers, rows...  23.1 us
    pallas_call x1, Pallas kernels, forward_line(): pl.pallas_call(forward_kernel, out_shape=(shape, shape), in_specs=[pl.Blo...  8.48 us

profile of v7, /device:TPU:6, one launch (start us, length us, event | category | flops | bytes accessed | tf_op | source)
XLA Modules:
  0.0 114.5 jit_solution(3068254767404418339)
XLA Ops:
  0.6 23.1 %shard_map.50 = bf16[32,108,128]{2,1,0:T(8,128)(2,1)} custom-call(bf16[108,128]{1,0:T(8,128)(2,1)} %bitcast.11), custom_call_target="tpu_custom_call" | custom-call | tf_op jit(solution)/shard_map/pallas_call | solution.py:85
  23.7 2.1 %reshape.10.w_ref = bf16[27,128,128]{2,1,0:T(8,128)(2,1)} reshape(bf16[32,108,128]{2,1,0:T(8,128)(2,1)} %shard_map.50) | data formatting | bytes 1769472 | tf_op jit(solution)/shard_map/reshape | solution.py:333
  25.8 8.5 %shard_map.51 = (bf16[8,256,128]{2,1,0:T(8,128)(2,1)}, bf16[8,256,128]{2,1,0:T(8,128)(2,1)}) custom-call(bf16[8,256,128]{2,1,0:T(8,128)(2,1)} %bitcast.9, bf16[27,128,128]{2,1,0:T(8,128)(2,1)} %reshape.10.w_ref), custom_call_target="tpu_custom_call" | custom-call | tf_op jit(solution)/shard_map/pallas_call | solution.py:243
  34.3 50.6 %shard_map.52 = f32[27,128,128]{2,1,0:T(8,128)} custom-call(bf16[8,256,128]{2,1,0:T(8,128)(2,1)} %bitcast.7, bf16[8,256,128]{2,1,0:T(8,128)(2,1)} %get-tuple-element.5.seen_ref, bf16[27,128,128]{2,1,0:T(8,128)(2,1)} %reshape.10.w_ref), custom_call_target="tpu_custom_call" | custom-call | tf_op jit(solution)/shard_map/pallas_call | solution.py:314
  84.9 1.6 %convert_element_type.3 = bf16[27,128,128]{2,1,0:T(8,128)(2,1)S(1)} convert(f32[27,128,128]{2,1,0:T(8,128)} %shard_map.52) | non-fusion elementwise | flops 442368 | bytes 2654208 | tf_op jit(solution)/shard_map/convert_element_type | solution.py:339
  86.5 0.0 copy-start
  86.5 1.1 reshape.11.parts_ref
  87.6 24.6 %shard_map.53 = f32[108,128]{1,0:T(8,128)} custom-call(bf16[32,108,128]{2,1,0:T(8,128)(2,1)} %reshape.11.parts_ref), custom_call_target="tpu_custom_call" | custom-call | tf_op jit(solution)/shard_map/pallas_call | solution.py:138
  112.2 1.5 %copy.8 = f32[1,108,128]{2,0,1:T(1,128)} copy(f32[1,108,128]{2,1,0:T(8,128)} %bitcast.10) | data formatting | bytes 110592
  113.7 0.0 copy-done
  113.7 0.8 copy.10
Async XLA Ops:
  86.5 27.2 %copy-start = (bf16[8,256,128]{2,1,0:T(8,128)(2,1)S(1)}, bf16[8,256,128]{2,1,0:T(8,128)(2,1)}, u32[]{:S(2)}) copy-start(bf16[8,256,128]{2,1,0:T(8,128)(2,1)} %get-tuple-element.4) | copy-start | bytes 1572868

commit v8 on v7

--- a/solution.py
+++ b/solution.py
@@ -159,7 +159,7 @@
     pad_ref[0:2, 1:9, 1:9, :] = jnp.broadcast_to(field[0:1], (2,) + field.shape[1:])
 
 
-def tap_windows(pad_ref, frames, flipped):
+def tap_windows(pad_ref, frames, flipped, start=0):
     channels = pad_ref.shape[-1]
     for c0 in range(3):
         shifted = pad_ref[:, :, c0 : c0 + 8, :]
@@ -168,7 +168,7 @@
             for offset_row in range(3):
                 t0 = 2 - offset_time if flipped else offset_time
                 r0 = 2 - offset_row if flipped else offset_row
-                window = shifted[t0 : t0 + frames, r0 : r0 + 8].reshape(frames * 64, channels)
+                window = shifted[start + t0 : start + t0 + frames, r0 : r0 + 8].reshape(frames * 64, channels)
                 yield offset_time * 9 + offset_row * 3 + offset_col, window.astype(jnp.bfloat16)
 
 
@@ -202,30 +202,42 @@
     count = lax.axis_size("section")
     here = lax.axis_index("section")
     col = lax.axis_index("dp")
-    micro_count = clips_ref.shape[0]
+    micro_count, cells, channels = clips_ref.shape
+    half = cells // 2
     greet_line(here, count, col)
     pad[...] = jnp.zeros_like(pad)
 
+    def hop(m, part, target):
+        rows = pl.ds(part * half, half)
+        return line_copy(out_ref.at[m, rows], recv.at[m, rows], send_sem.at[m, part], recv_sem.at[m, part], target, col)
+
     def step(m, carry):
-        @pl.when(here == 0)
-        def _():
-            seen_ref[m] = clips_ref[m]
-
-        @pl.when(here > 0)
-        def _():
-            line_copy(out_ref.at[m], recv.at[m], send_sem.at[m], recv_sem.at[m], here - 1, col).wait_recv()
-            seen_ref[m] = recv[m]
-
-        base = seen_ref[m].astype(jnp.float32)
-        squash_into(pad, base)
-        total = base
-        for tap, window in tap_windows(pad, 4, False):
-            total = total + jnp.dot(window, w_ref[tap], preferred_element_type=jnp.float32)
-        out_ref[m] = total.astype(out_ref.dtype)
-
-        @pl.when(here < count - 1)
-        def _():
-            line_copy(out_ref.at[m], recv.at[m], send_sem.at[m], recv_sem.at[m], here + 1, col).start()
+        for part in range(2):
+            rows = pl.ds(part * half, half)
+
+            @pl.when(here == 0)
+            def _():
+                seen_ref[m, rows] = clips_ref[m, rows]
+
+            @pl.when(here > 0)
+            def _():
+                hop(m, part, here - 1).wait_recv()
+                seen_ref[m, rows] = recv[m, rows]
+
+            base = seen_ref[m, rows].astype(jnp.float32)
+            squashed = (base / (1.0 + jnp.exp(-base))).astype(jnp.bfloat16).astype(jnp.float32)
+            field = squashed.reshape(2, 8, 8, channels)
+            pad[2 + 2 * part : 4 + 2 * part, 1:9, 1:9, :] = field
+            if part == 0:
+                pad[0:2, 1:9, 1:9, :] = jnp.broadcast_to(field[0:1], field.shape)
+            total = base
+            for tap, window in tap_windows(pad, 2, False, 2 * part):
+                total = total + jnp.dot(window, w_ref[tap], preferred_element_type=jnp.float32)
+            out_ref[m, rows] = total.astype(out_ref.dtype)
+
+            @pl.when(here < count - 1)
+            def _():
+                hop(m, part, here + 1).start()
 
         return carry
 
@@ -234,7 +246,8 @@
     @pl.when(here < count - 1)
     def _():
         for m in range(micro_count):
-            line_copy(out_ref.at[m], recv.at[m], send_sem.at[m], recv_sem.at[m], here + 1, col).wait_send()
+            for part in range(2):
+                hop(m, part, here + 1).wait_send()
 
 
 def forward_line(clips_local, weight):
@@ -248,8 +261,8 @@
         scratch_shapes=[
             pltpu.VMEM(clips_local.shape, clips_local.dtype),
             pltpu.VMEM((cells // 64 + 2, 10, 10, channels), jnp.float32),
-            pltpu.SemaphoreType.DMA((micro_count,)),
-            pltpu.SemaphoreType.DMA((micro_count,)),
+            pltpu.SemaphoreType.DMA((micro_count, 2)),
+            pltpu.SemaphoreType.DMA((micro_count, 2)),
         ],
         compiler_params=pltpu.CompilerParams(collective_id=2, has_side_effects=True),
     )(clips_local, weight)
@@ -259,40 +272,52 @@
     count = lax.axis_size("section")
     here = lax.axis_index("section")
     col = lax.axis_index("dp")
-    micro_count = cot_ref.shape[0]
+    micro_count, cells, channels = cot_ref.shape
+    half = cells // 2
     greet_line(here, count, col)
     pad[...] = jnp.zeros_like(pad)
     gpad[...] = jnp.zeros_like(gpad)
     wg_ref[...] = jnp.zeros_like(wg_ref)
 
+    def hop(m, part, target):
+        rows = pl.ds(part * half, half)
+        return line_copy(sendbuf.at[m, rows], recv.at[m, rows], send_sem.at[m, part], recv_sem.at[m, part], target, col)
+
     def step(m, carry):
-        @pl.when(here == count - 1)
-        def _():
-            recv[m] = cot_ref[m]
-
-        @pl.when(here < count - 1)
-        def _():
-            line_copy(sendbuf.at[m], recv.at[m], send_sem.at[m], recv_sem.at[m], here + 1, col).wait_recv()
+        for part in (1, 0):
+            rows = pl.ds(part * half, half)
+
+            @pl.when(here == count - 1)
+            def _():
+                recv[m, rows] = cot_ref[m, rows]
+
+            @pl.when(here < count - 1)
+            def _():
+                hop(m, part, here + 1).wait_recv()
+
+            @pl.when(here > 0)
+            def _():
+                up = recv[m, rows].astype(jnp.float32)
+                gpad[2 + 2 * part : 4 + 2 * part, 1:9, 1:9, :] = up.reshape(2, 8, 8, channels)
+                frames = 2 if part else 4
+                spread = jnp.zeros((frames * 64, channels), jnp.float32)
+                for tap, window in tap_windows(gpad, frames, True, 4 if part else 0):
+                    spread = spread + lax.dot_general(
+                        window, w_ref[tap], (((1,), (1,)), ((), ())),
+                        preferred_element_type=jnp.float32,
+                    )
+                if part:
+                    field = spread
+                else:
+                    field = jnp.concatenate([spread[0:64] + spread[64:128] + spread[128:192], spread[192:256]], axis=0)
+                base = seen_ref[m, rows].astype(jnp.float32)
+                sig = 1.0 / (1.0 + jnp.exp(-base))
+                slope = sig * (1.0 + base * (1.0 - sig))
+                sendbuf[m, rows] = (up + field * slope).astype(sendbuf.dtype)
+                hop(m, part, here - 1).start()
 
         upstream = recv[m]
-        base = seen_ref[m].astype(jnp.float32)
-        squash_into(pad, base)
-        @pl.when(here > 0)
-        def _():
-            up = upstream.astype(jnp.float32)
-            gpad[2:6, 1:9, 1:9, :] = up.reshape(4, 8, 8, up.shape[-1])
-            spread = jnp.zeros((384, up.shape[-1]), jnp.float32)
-            for tap, window in tap_windows(gpad, 6, True):
-                spread = spread + lax.dot_general(
-                    window, w_ref[tap], (((1,), (1,)), ((), ())),
-                    preferred_element_type=jnp.float32,
-                )
-            field = jnp.concatenate([spread[0:64] + spread[64:128] + spread[128:192], spread[192:384]], axis=0)
-            sig = 1.0 / (1.0 + jnp.exp(-base))
-            slope = sig * (1.0 + base * (1.0 - sig))
-            sendbuf[m] = (up + field * slope).astype(sendbuf.dtype)
-            line_copy(sendbuf.at[m], recv.at[m], send_sem.at[m], recv_sem.at[m], here - 1, col).start()
-
+        squash_into(pad, seen_ref[m].astype(jnp.float32))
         for tap, window in tap_windows(pad, 4, False):
             wg_ref[tap] += lax.dot_general(
                 window, upstream, (((0,), (0,)), ((), ())),
@@ -305,7 +330,8 @@
     @pl.when(here > 0)
     def _():
         for m in range(micro_count):
-            line_copy(sendbuf.at[m], recv.at[m], send_sem.at[m], recv_sem.at[m], here - 1, col).wait_send()
+            for part in range(2):
+                hop(m, part, here - 1).wait_send()
 
 
 def backward_line(cot_local, seen, weight):
@@ -321,8 +347,8 @@
             pltpu.VMEM(cot_local.shape, cot_local.dtype),
             pltpu.VMEM((cells // 64 + 2, 10, 10, channels), jnp.float32),
             pltpu.VMEM((cells // 64 + 4, 10, 10, channels), jnp.float32),
-            pltpu.SemaphoreType.DMA((micro_count,)),
-            pltpu.SemaphoreType.DMA((micro_count,)),
+            pltpu.SemaphoreType.DMA((micro_count, 2)),
+            pltpu.SemaphoreType.DMA((micro_count, 2)),
         ],
         compiler_params=pltpu.CompilerParams(collective_id=3, has_side_effects=True),
     )(cot_local, seen, weight)

time: 115 us -> 119 us (1.035)
  Pallas kernels: 107 us -> 111 us
    pallas_call x1, Pallas kernels: 8.48 us -> 13.1 us  [forward_line(): pl.pallas_call(forward_kernel, out_shape=(shape, shape), in_specs=[pl.Blo...]
where the time goes in v8:
time: 119 us
  Pallas kernels  111 us (93%)
  local copies, waits for them, and re-layouts  5.45 us (5%)
  other arithmetic  1.63 us (1%)
    pallas_call x1, Pallas kernels, backward_line(): pl.pallas_call(backward_kernel, out_shape=jax.ShapeDtypeStruct((taps, cha...  50.3 us
    pallas_call x1, Pallas kernels, scatter_rows(): pl.pallas_call(scatter_kernel, out_shape=jax.ShapeDtypeStruct((rows, cols...  24.6 us
    pallas_call x1, Pallas kernels, gather_rows(): pl.pallas_call(gather_kernel, out_shape=jax.ShapeDtypeStruct((peers, rows...  23.1 us
    pallas_call x1, Pallas kernels, forward_line(): pl.pallas_call(forward_kernel, out_shape=(shape, shape), in_specs=[pl.Blo...  13.1 us

profile of v8, /device:TPU:6, one launch (start us, length us, event | category | flops | bytes accessed | tf_op | source)
XLA Modules:
  0.0 118.9 jit_solution(12265523056296767980)
XLA Ops:
  0.6 23.1 %shard_map.50 = bf16[32,108,128]{2,1,0:T(8,128)(2,1)} custom-call(bf16[108,128]{1,0:T(8,128)(2,1)} %bitcast.11), custom_call_target="tpu_custom_call" | custom-call | tf_op jit(solution)/shard_map/pallas_call | solution.py:85
  23.7 2.1 %reshape.10.w_ref = bf16[27,128,128]{2,1,0:T(8,128)(2,1)} reshape(bf16[32,108,128]{2,1,0:T(8,128)(2,1)} %shard_map.50) | data formatting | bytes 1769472 | tf_op jit(solution)/shard_map/reshape | solution.py:359
  25.8 13.1 %shard_map.51 = (bf16[8,256,128]{2,1,0:T(8,128)(2,1)}, bf16[8,256,128]{2,1,0:T(8,128)(2,1)}) custom-call(bf16[8,256,128]{2,1,0:T(8,128)(2,1)} %bitcast.9, bf16[27,128,128]{2,1,0:T(8,128)(2,1)} %reshape.10.w_ref), custom_call_target="tpu_custom_call" | custom-call | tf_op jit(solution)/shard_map/pallas_call | solution.py:256
  39.0 50.3 %shard_map.52 = f32[27,128,128]{2,1,0:T(8,128)} custom-call(bf16[8,256,128]{2,1,0:T(8,128)(2,1)} %bitcast.7, bf16[8,256,128]{2,1,0:T(8,128)(2,1)} %get-tuple-element.5.seen_ref, bf16[27,128,128]{2,1,0:T(8,128)(2,1)} %reshape.10.w_ref), custom_call_target="tpu_custom_call" | custom-call | tf_op jit(solution)/shard_map/pallas_call | solution.py:340
  89.2 1.6 %convert_element_type.3 = bf16[27,128,128]{2,1,0:T(8,128)(2,1)S(1)} convert(f32[27,128,128]{2,1,0:T(8,128)} %shard_map.52) | non-fusion elementwise | flops 442368 | bytes 2654208 | tf_op jit(solution)/shard_map/convert_element_type | solution.py:365
  90.9 0.0 copy-start
  90.9 1.1 reshape.11.parts_ref
  92.0 24.6 %shard_map.53 = f32[108,128]{1,0:T(8,128)} custom-call(bf16[32,108,128]{2,1,0:T(8,128)(2,1)} %reshape.11.parts_ref), custom_call_target="tpu_custom_call" | custom-call | tf_op jit(solution)/shard_map/pallas_call | solution.py:138
  116.6 1.5 %copy.8 = f32[1,108,128]{2,0,1:T(1,128)} copy(f32[1,108,128]{2,1,0:T(8,128)} %bitcast.10) | data formatting | bytes 110592
  118.1 0.0 copy-done
  118.1 0.8 copy.10
Async XLA Ops:
  90.9 27.2 %copy-start = (bf16[8,256,128]{2,1,0:T(8,128)(2,1)S(1)}, bf16[8,256,128]{2,1,0:T(8,128)(2,1)}, u32[]{:S(2)}) copy-start(bf16[8,256,128]{2,1,0:T(8,128)(2,1)} %get-tuple-element.4) | copy-start | bytes 1572868

commit v9 on v7

--- a/solution.py
+++ b/solution.py
@@ -161,6 +161,7 @@
 
 def tap_windows(pad_ref, frames, flipped):
     channels = pad_ref.shape[-1]
+    windows = {}
     for c0 in range(3):
         shifted = pad_ref[:, :, c0 : c0 + 8, :]
         offset_col = 2 - c0 if flipped else c0
@@ -169,7 +170,11 @@
                 t0 = 2 - offset_time if flipped else offset_time
                 r0 = 2 - offset_row if flipped else offset_row
                 window = shifted[t0 : t0 + frames, r0 : r0 + 8].reshape(frames * 64, channels)
-                yield offset_time * 9 + offset_row * 3 + offset_col, window.astype(jnp.bfloat16)
+                windows[offset_time * 9 + offset_row * 3 + offset_col] = window.astype(jnp.bfloat16)
+    taps = len(windows)
+    for first in range(0, taps, 2):
+        group = [windows[tap] for tap in range(first, min(first + 2, taps))]
+        yield first, len(group), jnp.concatenate(group, axis=1) if len(group) > 1 else group[0]
 
 
 def greet_line(here, count, col):
@@ -202,7 +207,7 @@
     count = lax.axis_size("section")
     here = lax.axis_index("section")
     col = lax.axis_index("dp")
-    micro_count = clips_ref.shape[0]
+    micro_count, _, channels = clips_ref.shape
     greet_line(here, count, col)
     pad[...] = jnp.zeros_like(pad)
 
@@ -219,8 +224,9 @@
         base = seen_ref[m].astype(jnp.float32)
         squash_into(pad, base)
         total = base
-        for tap, window in tap_windows(pad, 4, False):
-            total = total + jnp.dot(window, w_ref[tap], preferred_element_type=jnp.float32)
+        for tap, width, window in tap_windows(pad, 4, False):
+            rows = pl.ds(tap * channels, width * channels)
+            total = total + jnp.dot(window, w_ref[rows, :], preferred_element_type=jnp.float32)
         out_ref[m] = total.astype(out_ref.dtype)
 
         @pl.when(here < count - 1)
@@ -259,7 +265,7 @@
     count = lax.axis_size("section")
     here = lax.axis_index("section")
     col = lax.axis_index("dp")
-    micro_count = cot_ref.shape[0]
+    micro_count, _, channels = cot_ref.shape
     greet_line(here, count, col)
     pad[...] = jnp.zeros_like(pad)
     gpad[...] = jnp.zeros_like(gpad)
@@ -282,9 +288,10 @@
             up = upstream.astype(jnp.float32)
             gpad[2:6, 1:9, 1:9, :] = up.reshape(4, 8, 8, up.shape[-1])
             spread = jnp.zeros((384, up.shape[-1]), jnp.float32)
-            for tap, window in tap_windows(gpad, 6, True):
+            for tap, width, window in tap_windows(gpad, 6, True):
+                paired = jnp.concatenate([w_ref[pl.ds((tap + k) * channels, channels), :] for k in range(width)], axis=1)
                 spread = spread + lax.dot_general(
-                    window, w_ref[tap], (((1,), (1,)), ((), ())),
+                    window, paired, (((1,), (1,)), ((), ())),
                     preferred_element_type=jnp.float32,
                 )
             field = jnp.concatenate([spread[0:64] + spread[64:128] + spread[128:192], spread[192:384]], axis=0)
@@ -293,8 +300,8 @@
             sendbuf[m] = (up + field * slope).astype(sendbuf.dtype)
             line_copy(sendbuf.at[m], recv.at[m], send_sem.at[m], recv_sem.at[m], here - 1, col).start()
 
-        for tap, window in tap_windows(pad, 4, False):
-            wg_ref[tap] += lax.dot_general(
+        for tap, width, window in tap_windows(pad, 4, False):
+            wg_ref[pl.ds(tap * channels, width * channels), :] += lax.dot_general(
                 window, upstream, (((0,), (0,)), ((), ())),
                 preferred_element_type=jnp.float32,
             )
@@ -310,10 +317,9 @@
 
 def backward_line(cot_local, seen, weight):
     micro_count, cells, channels = cot_local.shape
-    taps = weight.shape[0]
     return pl.pallas_call(
         backward_kernel,
-        out_shape=jax.ShapeDtypeStruct((taps, channels, channels), jnp.float32),
+        out_shape=jax.ShapeDtypeStruct(weight.shape, jnp.float32),
         in_specs=[pl.BlockSpec(memory_space=pltpu.VMEM)] * 3,
         out_specs=pl.BlockSpec(memory_space=pltpu.VMEM),
         scratch_shapes=[
@@ -330,7 +336,7 @@
 
 def per_device(clips, cotangent, weights):
     channels = weights.shape[-1]
-    weight = gather_rows(weights[0]).reshape(-1, channels, channels)
+    weight = gather_rows(weights[0]).reshape(-1, channels)
     micro_count = clips.shape[0]
     clips_local = clips[:, 0].reshape(micro_count, -1, channels)
     cot_local = cotangent[:, 0].reshape(micro_count, -1, channels)

time: 115 us -> 115 us (level)
  no operation moved by 1% of the time
where the time goes in v9:
time: 115 us
  Pallas kernels  107 us (93%)
  local copies, waits for them, and re-layouts  5.45 us (5%)
  other arithmetic  1.56 us (1%)
    pallas_call x1, Pallas kernels, backward_line(): pl.pallas_call(backward_kernel, out_shape=jax.ShapeDtypeStruct(weight.sha...  51.2 us
    pallas_call x1, Pallas kernels, scatter_rows(): pl.pallas_call(scatter_kernel, out_shape=jax.ShapeDtypeStruct((rows, cols...  24.5 us
    pallas_call x1, Pallas kernels, gather_rows(): pl.pallas_call(gather_kernel, out_shape=jax.ShapeDtypeStruct((peers, rows...  23.1 us
    pallas_call x1, Pallas kernels, forward_line(): pl.pallas_call(forward_kernel, out_shape=(shape, shape), in_specs=[pl.Blo...  8.67 us

profile of v9, /device:TPU:6, one launch (start us, length us, event | category | flops | bytes accessed | tf_op | source)
XLA Modules:
  0.0 115.1 jit_solution(15244555907442956016)
XLA Ops:
  0.6 23.1 %shard_map.50 = bf16[32,108,128]{2,1,0:T(8,128)(2,1)} custom-call(bf16[108,128]{1,0:T(8,128)(2,1)} %bitcast.11), custom_call_target="tpu_custom_call" | custom-call | tf_op jit(solution)/shard_map/pallas_call | solution.py:85
  23.7 2.1 %reshape.10.w_ref = bf16[3456,128]{1,0:T(8,128)(2,1)} reshape(bf16[32,108,128]{2,1,0:T(8,128)(2,1)} %shard_map.50) | data formatting | bytes 1769472 | tf_op jit(solution)/shard_map/reshape | solution.py:339
  25.8 8.7 %shard_map.51 = (bf16[8,256,128]{2,1,0:T(8,128)(2,1)}, bf16[8,256,128]{2,1,0:T(8,128)(2,1)}) custom-call(bf16[8,256,128]{2,1,0:T(8,128)(2,1)} %bitcast.9, bf16[3456,128]{1,0:T(8,128)(2,1)} %reshape.10.w_ref), custom_call_target="tpu_custom_call" | custom-call | tf_op jit(solution)/shard_map/pallas_call | solution.py:249
  34.5 51.2 %shard_map.52 = f32[3456,128]{1,0:T(8,128)} custom-call(bf16[8,256,128]{2,1,0:T(8,128)(2,1)} %bitcast.7, bf16[8,256,128]{2,1,0:T(8,128)(2,1)} %get-tuple-element.5.seen_ref, bf16[3456,128]{1,0:T(8,128)(2,1)} %reshape.10.w_ref), custom_call_target="tpu_custom_call" | custom-call | tf_op jit(solution)/shard_map/pallas_call | solution.py:320
  85.6 1.6 %convert_element_type.3 = bf16[3456,128]{1,0:T(8,128)(2,1)S(1)} convert(f32[3456,128]{1,0:T(8,128)} %shard_map.52) | non-fusion elementwise | flops 442368 | bytes 2654208 | tf_op jit(solution)/shard_map/convert_element_type | solution.py:345
  87.2 0.0 copy-start
  87.2 1.1 reshape.11.parts_ref
  88.3 24.5 %shard_map.53 = f32[108,128]{1,0:T(8,128)} custom-call(bf16[32,108,128]{2,1,0:T(8,128)(2,1)} %reshape.11.parts_ref), custom_call_target="tpu_custom_call" | custom-call | tf_op jit(solution)/shard_map/pallas_call | solution.py:138
  112.8 1.5 %copy.8 = f32[1,108,128]{2,0,1:T(1,128)} copy(f32[1,108,128]{2,1,0:T(8,128)} %bitcast.10) | data formatting | bytes 110592
  114.3 0.0 copy-done
  114.3 0.8 copy.10
Async XLA Ops:
  87.2 27.1 %copy-start = (bf16[8,256,128]{2,1,0:T(8,128)(2,1)S(1)}, bf16[8,256,128]{2,1,0:T(8,128)(2,1)}, u32[]{:S(2)}) copy-start(bf16[8,256,128]{2,1,0:T(8,128)(2,1)} %get-tuple-element.4) | copy-start | bytes 1572868

commit v10 on v7

--- a/solution.py
+++ b/solution.py
@@ -37,7 +37,7 @@
     )
 
 
-def gather_kernel(shard_ref, out_ref, send_sem, recv_sem):
+def gather_kernel(shard_ref, flat_ref, out_ref, send_sem, recv_sem):
     peers = lax.axis_size("dp")
     here = lax.axis_index("dp")
     row = lax.axis_index("section")
@@ -77,6 +77,9 @@
         return carry
 
     lax.fori_loop(1, planes, finish, 0)
+    rows = shard_ref.shape[0]
+    for block in range(peers):
+        flat_ref[block * rows : (block + 1) * rows, :] = out_ref[block]
 
 
 def gather_rows(shard):
@@ -84,10 +87,14 @@
     rows, cols = shard.shape
     return pl.pallas_call(
         gather_kernel,
-        out_shape=jax.ShapeDtypeStruct((peers, rows, cols), shard.dtype),
+        out_shape=jax.ShapeDtypeStruct((peers * rows, cols), shard.dtype),
         in_specs=[pl.BlockSpec(memory_space=pltpu.VMEM)],
         out_specs=pl.BlockSpec(memory_space=pltpu.VMEM),
-        scratch_shapes=[pltpu.SemaphoreType.DMA((peers,)), pltpu.SemaphoreType.DMA((peers,))],
+        scratch_shapes=[
+            pltpu.VMEM((peers, rows, cols), shard.dtype),
+            pltpu.SemaphoreType.DMA((peers,)),
+            pltpu.SemaphoreType.DMA((peers,)),
+        ],
         compiler_params=pltpu.CompilerParams(collective_id=0, has_side_effects=True),
     )(shard)
 
@@ -255,7 +262,7 @@
     )(clips_local, weight)
 
 
-def backward_kernel(cot_ref, seen_ref, w_ref, wg_ref, recv, sendbuf, pad, gpad, send_sem, recv_sem):
+def backward_kernel(cot_ref, seen_ref, w_ref, parts_ref, recv, sendbuf, pad, gpad, wg_ref, send_sem, recv_sem):
     count = lax.axis_size("section")
     here = lax.axis_index("section")
     col = lax.axis_index("dp")
@@ -294,13 +301,17 @@
             line_copy(sendbuf.at[m], recv.at[m], send_sem.at[m], recv_sem.at[m], here - 1, col).start()
 
         for tap, window in tap_windows(pad, 4, False):
-            wg_ref[tap] += lax.dot_general(
+            wg_ref[tap * 128 : (tap + 1) * 128, :] += lax.dot_general(
                 window, upstream, (((0,), (0,)), ((), ())),
                 preferred_element_type=jnp.float32,
             )
         return carry
 
     lax.fori_loop(0, micro_count, step, 0)
+
+    block_rows = parts_ref.shape[1]
+    for block in range(parts_ref.shape[0]):
+        parts_ref[block] = wg_ref[block * block_rows : (block + 1) * block_rows, :].astype(parts_ref.dtype)
 
     @pl.when(here > 0)
     def _():
@@ -308,12 +319,12 @@
             line_copy(sendbuf.at[m], recv.at[m], send_sem.at[m], recv_sem.at[m], here - 1, col).wait_send()
 
 
-def backward_line(cot_local, seen, weight):
+def backward_line(cot_local, seen, weight, blocks):
     micro_count, cells, channels = cot_local.shape
     taps = weight.shape[0]
     return pl.pallas_call(
         backward_kernel,
-        out_shape=jax.ShapeDtypeStruct((taps, channels, channels), jnp.float32),
+        out_shape=jax.ShapeDtypeStruct((blocks, taps * channels // blocks, channels), jnp.bfloat16),
         in_specs=[pl.BlockSpec(memory_space=pltpu.VMEM)] * 3,
         out_specs=pl.BlockSpec(memory_space=pltpu.VMEM),
         scratch_shapes=[
@@ -321,6 +332,7 @@
             pltpu.VMEM(cot_local.shape, cot_local.dtype),
             pltpu.VMEM((cells // 64 + 2, 10, 10, channels), jnp.float32),
             pltpu.VMEM((cells // 64 + 4, 10, 10, channels), jnp.float32),
+            pltpu.VMEM((taps * channels, channels), jnp.float32),
             pltpu.SemaphoreType.DMA((micro_count,)),
             pltpu.SemaphoreType.DMA((micro_count,)),
         ],
@@ -331,12 +343,12 @@
 def per_device(clips, cotangent, weights):
     channels = weights.shape[-1]
     weight = gather_rows(weights[0]).reshape(-1, channels, channels)
+    blocks = lax.axis_size("dp")
     micro_count = clips.shape[0]
     clips_local = clips[:, 0].reshape(micro_count, -1, channels)
     cot_local = cotangent[:, 0].reshape(micro_count, -1, channels)
     seen, produced = forward_line(clips_local, weight)
-    grad_total = backward_line(cot_local, seen, weight)
-    grad_share = scatter_rows(grad_total.astype(jnp.bfloat16).reshape(lax.axis_size("dp"), -1, channels))
+    grad_share = scatter_rows(backward_line(cot_local, seen, weight, blocks))
     return (produced.reshape(clips[:, 0].shape)[None, :, None], grad_share[None])
 
 

time: 115 us -> 110 us (0.957)
  local copies, waits for them, and re-layouts: 5.45 us -> 2.3 us
  other arithmetic: 1.63 us -> 0 us
    reshape x2 -> x0, local copies, waits for them, and re-layouts: 3.15 us -> none  [the longest x1 2.08 us: per_device(): weight = gather_rows(weights[0]).reshape(-1, channels, channels)]
    convert_element_type x1 -> x0, other arithmetic: 1.63 us -> none  [per_device(): grad_total.astype(jnp.bfloat16).reshape(lax.axis_size('dp'), -1, channels)]
where the time goes in v10:
time: 110 us
  Pallas kernels  107 us (97%)
  local copies, waits for them, and re-layouts  2.3 us (2%)
    pallas_call x1, Pallas kernels, backward_line(): pl.pallas_call(backward_kernel, out_shape=jax.ShapeDtypeStruct((blocks, t...  50.3 us
    pallas_call x1, Pallas kernels, scatter_rows(): pl.pallas_call(scatter_kernel, out_shape=jax.ShapeDtypeStruct((rows, cols...  24.6 us
    pallas_call x1, Pallas kernels, gather_rows(): pl.pallas_call(gather_kernel, out_shape=jax.ShapeDtypeStruct((peers * row...  23.3 us
    pallas_call x1, Pallas kernels, forward_line(): pl.pallas_call(forward_kernel, out_shape=(shape, shape), in_specs=[pl.Blo...  8.61 us
    unnamed x4, local copies, waits for them, and re-layouts  2.3 us

profile of v10, /device:TPU:6, one launch (start us, length us, event | category | flops | bytes accessed | tf_op | source)
XLA Modules:
  0.0 109.8 jit_solution(14960780309030737193)
XLA Ops:
  0.6 23.3 %shard_map.50 = bf16[3456,128]{1,0:T(8,128)(2,1)} custom-call(bf16[108,128]{1,0:T(8,128)(2,1)} %bitcast.14), custom_call_target="tpu_custom_call" | custom-call | tf_op jit(solution)/shard_map/pallas_call | solution.py:88
  23.9 8.6 %shard_map.51 = (bf16[8,256,128]{2,1,0:T(8,128)(2,1)}, bf16[8,256,128]{2,1,0:T(8,128)(2,1)}) custom-call(bf16[8,256,128]{2,1,0:T(8,128)(2,1)} %bitcast.11, bf16[27,128,128]{2,1,0:T(8,128)(2,1)} %bitcast.8), custom_call_target="tpu_custom_call" | custom-call | tf_op jit(solution)/shard_map/pallas_call | solution.py:250
  32.5 50.3 %shard_map.52.parts_ref = bf16[32,108,128]{2,1,0:T(8,128)(2,1)} custom-call(bf16[8,256,128]{2,1,0:T(8,128)(2,1)} %bitcast.12, bf16[8,256,128]{2,1,0:T(8,128)(2,1)} %get-tuple-element.5.seen_ref, bf16[27,128,128]{2,1,0:T(8,128)(2,1)} %bitcast.9), custom_call_target="tpu_custom_call" | custom-call | tf_op jit(solution)/shard_map/pallas_call | solution.py:325
  82.9 0.0 copy-start
  82.9 24.6 %shard_map.53 = f32[108,128]{1,0:T(8,128)} custom-call(bf16[32,108,128]{2,1,0:T(8,128)(2,1)} %shard_map.52.parts_ref), custom_call_target="tpu_custom_call" | custom-call | tf_op jit(solution)/shard_map/pallas_call | solution.py:145
  107.5 1.5 %copy.6 = f32[1,108,128]{2,0,1:T(1,128)} copy(f32[1,108,128]{2,1,0:T(8,128)} %bitcast.13) | data formatting | bytes 110592
  109.0 0.0 copy-done
  109.0 0.8 copy.8
Async XLA Ops:
  82.9 26.1 %copy-start = (bf16[8,256,128]{2,1,0:T(8,128)(2,1)S(1)}, bf16[8,256,128]{2,1,0:T(8,128)(2,1)}, u32[]{:S(2)}) copy-start(bf16[8,256,128]{2,1,0:T(8,128)(2,1)} %get-tuple-element.4) | copy-start | bytes 1572868

commit v11 on v10

--- a/solution.py
+++ b/solution.py
@@ -112,32 +112,37 @@
         return group_copy(parts_ref.at[2 * (peer // 2) + block], held.at[slot, block],
                           send_sem.at[peer // 2, block], recv_sem.at[slot, block], row, peer)
 
-    def start(i, carry):
-        peer = lax.rem(here + 2 * i, peers)
-        fan(peer, 0).start()
-        fan(peer, 1).start()
-        return carry
-
-    lax.fori_loop(1, planes, start, 0)
-
-    def finish(i, totals):
-        peer = lax.rem(here + 2 * i, peers)
-        fan(peer, 0).wait_send()
-        fan(peer, 1).wait_send()
-        source = peer // 2
-        for block in range(2):
+    far = 1 - side
+
+    def start_far(i, carry):
+        fan(lax.rem(here + 2 * i, peers), far).start()
+        return carry
+
+    def start_near(i, carry):
+        fan(lax.rem(here + 2 * i, peers), side).start()
+        return carry
+
+    lax.fori_loop(1, planes, start_far, 0)
+    lax.fori_loop(1, planes, start_near, 0)
+
+    def gather_block(block):
+        def finish(i, total):
+            peer = lax.rem(here + 2 * i, peers)
+            fan(peer, block).wait_send()
+            source = peer // 2
             group_copy(parts_ref.at[block], held.at[source, block], send_sem.at[source, block],
                        recv_sem.at[source, block], row, peer).wait_recv()
-        return (totals[0] + held[source, 0].astype(jnp.float32), totals[1] + held[source, 1].astype(jnp.float32))
-
-    start_totals = (parts_ref[2 * slot].astype(jnp.float32), parts_ref[2 * slot + 1].astype(jnp.float32))
-    first, second = lax.fori_loop(1, planes, finish, start_totals)
-    theirs[...] = jnp.where(side == 0, second, first)
+            return total + held[source, block].astype(jnp.float32)
+
+        return lax.fori_loop(1, planes, finish, parts_ref[2 * slot + block].astype(jnp.float32))
+
+    theirs[...] = gather_block(far)
     cross = group_copy(theirs, mine, cross_sem.at[0], cross_sem.at[1], row, partner)
     cross.start()
+    own = gather_block(side)
     cross.wait_send()
     cross.wait_recv()
-    out_ref[...] = jnp.where(side == 0, first, second) + mine[...]
+    out_ref[...] = own + mine[...]
 
 
 def scatter_rows(parts):

time: 110 us -> 107 us (0.973)
  Pallas kernels: 107 us -> 103 us
    pallas_call x1, Pallas kernels: 24.6 us -> 20.7 us  [scatter_rows(): pl.pallas_call(scatter_kernel, out_shape=jax.ShapeDtypeStruct((rows, cols...]
where the time goes in v11:
time: 107 us; the launch traced here: 106 us
  Pallas kernels  103 us (96%)
  local copies, waits for them, and re-layouts  2.3 us (2%)
    pallas_call x1, Pallas kernels, backward_line(): pl.pallas_call(backward_kernel, out_shape=jax.ShapeDtypeStruct((blocks, t...  50.6 us
    pallas_call x1, Pallas kernels, gather_rows(): pl.pallas_call(gather_kernel, out_shape=jax.ShapeDtypeStruct((peers * row...  23.3 us
    pallas_call x1, Pallas kernels, scatter_rows(): pl.pallas_call(scatter_kernel, out_shape=jax.ShapeDtypeStruct((rows, cols...  20.7 us
    pallas_call x1, Pallas kernels, forward_line(): pl.pallas_call(forward_kernel, out_shape=(shape, shape), in_specs=[pl.Blo...  8.61 us
    unnamed x4, local copies, waits for them, and re-layouts  2.3 us

profile of v11, /device:TPU:6, one launch (start us, length us, event | category | flops | bytes accessed | tf_op | source)
XLA Modules:
  0.0 106.1 jit_solution(17147141813801199084)
XLA Ops:
  0.6 23.3 %shard_map.50 = bf16[3456,128]{1,0:T(8,128)(2,1)} custom-call(bf16[108,128]{1,0:T(8,128)(2,1)} %bitcast.14), custom_call_target="tpu_custom_call" | custom-call | tf_op jit(solution)/shard_map/pallas_call | solution.py:88
  23.9 8.6 %shard_map.51 = (bf16[8,256,128]{2,1,0:T(8,128)(2,1)}, bf16[8,256,128]{2,1,0:T(8,128)(2,1)}) custom-call(bf16[8,256,128]{2,1,0:T(8,128)(2,1)} %bitcast.11, bf16[27,128,128]{2,1,0:T(8,128)(2,1)} %bitcast.8), custom_call_target="tpu_custom_call" | custom-call | tf_op jit(solution)/shard_map/pallas_call | solution.py:255
  32.5 50.6 %shard_map.52.parts_ref = bf16[32,108,128]{2,1,0:T(8,128)(2,1)} custom-call(bf16[8,256,128]{2,1,0:T(8,128)(2,1)} %bitcast.12, bf16[8,256,128]{2,1,0:T(8,128)(2,1)} %get-tuple-element.5.seen_ref, bf16[27,128,128]{2,1,0:T(8,128)(2,1)} %bitcast.9), custom_call_target="tpu_custom_call" | custom-call | tf_op jit(solution)/shard_map/pallas_call | solution.py:330
  83.1 0.0 copy-start
  83.1 20.7 %shard_map.53 = f32[108,128]{1,0:T(8,128)} custom-call(bf16[32,108,128]{2,1,0:T(8,128)(2,1)} %shard_map.52.parts_ref), custom_call_target="tpu_custom_call" | custom-call | tf_op jit(solution)/shard_map/pallas_call | solution.py:150
  103.8 1.5 %copy.6 = f32[1,108,128]{2,0,1:T(1,128)} copy(f32[1,108,128]{2,1,0:T(8,128)} %bitcast.13) | data formatting | bytes 110592
  105.3 0.0 copy-done
  105.3 0.8 copy.8
Async XLA Ops:
  83.1 22.2 %copy-start = (bf16[8,256,128]{2,1,0:T(8,128)(2,1)S(1)}, bf16[8,256,128]{2,1,0:T(8,128)(2,1)}, u32[]{:S(2)}) copy-start(bf16[8,256,128]{2,1,0:T(8,128)(2,1)} %get-tuple-element.4) | copy-start | bytes 1572868

commit v12 on v11

--- a/solution.py
+++ b/solution.py
@@ -9,7 +9,7 @@
 MESH_ID = pl.DeviceIdType.MESH
 
 
-def greet_group(here, row):
+def greet_group(here, row, extra=0):
     pair = here - here % 2
     partner = pair + 1 - here % 2
     barrier = pltpu.get_barrier_semaphore()
@@ -22,7 +22,7 @@
 
     planes = lax.axis_size("dp") // 2
     lax.fori_loop(1, planes, signal, 0)
-    pl.semaphore_wait(barrier, planes)
+    pl.semaphore_wait(barrier, planes + extra)
     return partner
 
 
@@ -100,10 +100,15 @@
 
 
 def scatter_kernel(parts_ref, out_ref, held, mine, theirs, send_sem, recv_sem, cross_sem):
+    greet_group(lax.axis_index("dp"), lax.axis_index("section"))
+    scatter_blocks(parts_ref, out_ref, held, mine, theirs, send_sem, recv_sem, cross_sem)
+
+
+def scatter_blocks(parts_ref, out_ref, held, mine, theirs, send_sem, recv_sem, cross_sem):
     peers = lax.axis_size("dp")
     here = lax.axis_index("dp")
     row = lax.axis_index("section")
-    partner = greet_group(here, row)
+    partner = here - here % 2 + 1 - here % 2
     planes = peers // 2
     slot = here // 2
     side = here % 2
@@ -184,7 +189,7 @@
                 yield offset_time * 9 + offset_row * 3 + offset_col, window.astype(jnp.bfloat16)
 
 
-def greet_line(here, count, col):
+def greet_line(here, count, col, settle=True):
     barrier = pltpu.get_barrier_semaphore()
 
     @pl.when(here > 0)
@@ -196,7 +201,9 @@
         pl.semaphore_signal(barrier, inc=1, device_id=(here + 1, col), device_id_type=MESH_ID)
 
     neighbours = (here + count - 1) // count + (2 * count - 2 - here) // count
-    pl.semaphore_wait(barrier, neighbours)
+    if settle:
+        pl.semaphore_wait(barrier, neighbours)
+    return neighbours
 
 
 def line_copy(src, dst, send_sem, recv_sem, target, col):
@@ -267,12 +274,13 @@
     )(clips_local, weight)
 
 
-def backward_kernel(cot_ref, seen_ref, w_ref, parts_ref, recv, sendbuf, pad, gpad, wg_ref, send_sem, recv_sem):
+def backward_kernel(cot_ref, seen_ref, w_ref, share_ref, recv, sendbuf, pad, gpad, wg_ref, parts_ref, held, mine,
+                    theirs, send_sem, recv_sem, share_send, share_recv, cross_sem):
     count = lax.axis_size("section")
     here = lax.axis_index("section")
     col = lax.axis_index("dp")
     micro_count = cot_ref.shape[0]
-    greet_line(here, count, col)
+    greet_group(col, here, greet_line(here, count, col, settle=False))
     pad[...] = jnp.zeros_like(pad)
     gpad[...] = jnp.zeros_like(gpad)
     wg_ref[...] = jnp.zeros_like(wg_ref)
@@ -323,13 +331,16 @@
         for m in range(micro_count):
             line_copy(sendbuf.at[m], recv.at[m], send_sem.at[m], recv_sem.at[m], here - 1, col).wait_send()
 
+    scatter_blocks(parts_ref, share_ref, held, mine, theirs, share_send, share_recv, cross_sem)
+
 
 def backward_line(cot_local, seen, weight, blocks):
     micro_count, cells, channels = cot_local.shape
     taps = weight.shape[0]
+    block_rows = taps * channels // blocks
     return pl.pallas_call(
         backward_kernel,
-        out_shape=jax.ShapeDtypeStruct((blocks, taps * channels // blocks, channels), jnp.bfloat16),
+        out_shape=jax.ShapeDtypeStruct((block_rows, channels), jnp.float32),
         in_specs=[pl.BlockSpec(memory_space=pltpu.VMEM)] * 3,
         out_specs=pl.BlockSpec(memory_space=pltpu.VMEM),
         scratch_shapes=[
@@ -338,8 +349,15 @@
             pltpu.VMEM((cells // 64 + 2, 10, 10, channels), jnp.float32),
             pltpu.VMEM((cells // 64 + 4, 10, 10, channels), jnp.float32),
             pltpu.VMEM((taps * channels, channels), jnp.float32),
+            pltpu.VMEM((blocks, block_rows, channels), jnp.bfloat16),
+            pltpu.VMEM((blocks // 2, 2, block_rows, channels), jnp.bfloat16),
+            pltpu.VMEM((block_rows, channels), jnp.float32),
+            pltpu.VMEM((block_rows, channels), jnp.float32),
             pltpu.SemaphoreType.DMA((micro_count,)),
             pltpu.SemaphoreType.DMA((micro_count,)),
+            pltpu.SemaphoreType.DMA((blocks // 2, 2)),
+            pltpu.SemaphoreType.DMA((blocks // 2, 2)),
+            pltpu.SemaphoreType.DMA((2,)),
         ],
         compiler_params=pltpu.CompilerParams(collective_id=3, has_side_effects=True),
     )(cot_local, seen, weight)
@@ -353,7 +371,7 @@
     clips_local = clips[:, 0].reshape(micro_count, -1, channels)
     cot_local = cotangent[:, 0].reshape(micro_count, -1, channels)
     seen, produced = forward_line(clips_local, weight)
-    grad_share = scatter_rows(backward_line(cot_local, seen, weight, blocks))
+    grad_share = backward_line(cot_local, seen, weight, blocks)
     return (produced.reshape(clips[:, 0].shape)[None, :, None], grad_share[None])
 
 

time: 107 us -> 105 us (0.981)
    pallas_call x2 -> x1, Pallas kernels: 71.2 us -> 69.7 us  [backward_line(): pl.pallas_call(backward_kernel, out_shape=jax.ShapeDtypeStruct((block_row...]
where the time goes in v12:
time: 105 us
  Pallas kernels  102 us (97%)
  local copies, waits for them, and re-layouts  2.3 us (2%)
    pallas_call x1, Pallas kernels, backward_line(): pl.pallas_call(backward_kernel, out_shape=jax.ShapeDtypeStruct((block_row...  69.7 us
    pallas_call x1, Pallas kernels, gather_rows(): pl.pallas_call(gather_kernel, out_shape=jax.ShapeDtypeStruct((peers * row...  23.2 us
    pallas_call x1, Pallas kernels, forward_line(): pl.pallas_call(forward_kernel, out_shape=(shape, shape), in_specs=[pl.Blo...  8.61 us
    unnamed x4, local copies, waits for them, and re-layouts  2.3 us

profile of v12, /device:TPU:6, one launch (start us, length us, event | category | flops | bytes accessed | tf_op | source)
XLA Modules:
  0.0 104.5 jit_solution(3593739271977251350)
XLA Ops:
  0.6 23.2 %shard_map.50 = bf16[3456,128]{1,0:T(8,128)(2,1)} custom-call(bf16[108,128]{1,0:T(8,128)(2,1)} %bitcast.14), custom_call_target="tpu_custom_call" | custom-call | tf_op jit(solution)/shard_map/pallas_call | solution.py:88
  23.9 8.6 %shard_map.51 = (bf16[8,256,128]{2,1,0:T(8,128)(2,1)}, bf16[8,256,128]{2,1,0:T(8,128)(2,1)}) custom-call(bf16[8,256,128]{2,1,0:T(8,128)(2,1)} %bitcast.11, bf16[27,128,128]{2,1,0:T(8,128)(2,1)} %bitcast.8), custom_call_target="tpu_custom_call" | custom-call | tf_op jit(solution)/shard_map/pallas_call | solution.py:262
  32.5 0.0 copy-start
  32.5 69.7 %shard_map.52 = f32[108,128]{1,0:T(8,128)} custom-call(bf16[8,256,128]{2,1,0:T(8,128)(2,1)} %bitcast.12, bf16[8,256,128]{2,1,0:T(8,128)(2,1)} %get-tuple-element.5.seen_ref, bf16[27,128,128]{2,1,0:T(8,128)(2,1)} %bitcast.9), custom_call_target="tpu_custom_call" | custom-call | tf_op jit(solution)/shard_map/pallas_call | solution.py:341
  102.2 1.5 %copy.6 = f32[1,108,128]{2,0,1:T(1,128)} copy(f32[1,108,128]{2,1,0:T(8,128)} %bitcast.13) | data formatting | bytes 110592
  103.7 0.0 copy-done
  103.7 0.8 copy.8
Async XLA Ops:
  32.5 71.2 %copy-start = (bf16[8,256,128]{2,1,0:T(8,128)(2,1)S(1)}, bf16[8,256,128]{2,1,0:T(8,128)(2,1)}, u32[]{:S(2)}) copy-start(bf16[8,256,128]{2,1,0:T(8,128)(2,1)} %get-tuple-element.4) | copy-start | bytes 1572868

commit v13 on v12

--- a/solution.py
+++ b/solution.py
@@ -38,10 +38,15 @@
 
 
 def gather_kernel(shard_ref, flat_ref, out_ref, send_sem, recv_sem):
+    greet_group(lax.axis_index("dp"), lax.axis_index("section"))
+    gather_blocks(shard_ref, flat_ref, out_ref, send_sem, recv_sem)
+
+
+def gather_blocks(shard_ref, flat_ref, out_ref, send_sem, recv_sem):
     peers = lax.axis_size("dp")
     here = lax.axis_index("dp")
     row = lax.axis_index("section")
-    partner = greet_group(here, row)
+    partner = here - here % 2 + 1 - here % 2
     planes = peers // 2
     cross = group_copy(shard_ref, out_ref.at[here], send_sem.at[here], recv_sem.at[here], row, partner)
     cross.start()
@@ -217,13 +222,16 @@
     )
 
 
-def forward_kernel(clips_ref, w_ref, seen_ref, out_ref, recv, pad, send_sem, recv_sem):
+def forward_kernel(clips_ref, shard_ref, seen_ref, out_ref, flat_ref, recv, pad, blocks, gather_send, gather_recv,
+                   send_sem, recv_sem):
     count = lax.axis_size("section")
     here = lax.axis_index("section")
     col = lax.axis_index("dp")
     micro_count = clips_ref.shape[0]
-    greet_line(here, count, col)
+    greet_group(col, here, greet_line(here, count, col, settle=False))
     pad[...] = jnp.zeros_like(pad)
+    gather_blocks(shard_ref, flat_ref, blocks, gather_send, gather_recv)
+    channels = flat_ref.shape[-1]
 
     def step(m, carry):
         @pl.when(here == 0)
@@ -239,7 +247,9 @@
         squash_into(pad, base)
         total = base
         for tap, window in tap_windows(pad, 4, False):
-            total = total + jnp.dot(window, w_ref[tap], preferred_element_type=jnp.float32)
+            total = total + jnp.dot(
+                window, flat_ref[tap * channels : (tap + 1) * channels, :], preferred_element_type=jnp.float32
+            )
         out_ref[m] = total.astype(out_ref.dtype)
 
         @pl.when(here < count - 1)
@@ -256,22 +266,27 @@
             line_copy(out_ref.at[m], recv.at[m], send_sem.at[m], recv_sem.at[m], here + 1, col).wait_send()
 
 
-def forward_line(clips_local, weight):
+def forward_line(clips_local, shard):
     shape = jax.ShapeDtypeStruct(clips_local.shape, clips_local.dtype)
     micro_count, cells, channels = clips_local.shape
+    peers = lax.axis_size("dp")
+    rows = shard.shape[0]
     return pl.pallas_call(
         forward_kernel,
-        out_shape=(shape, shape),
+        out_shape=(shape, shape, jax.ShapeDtypeStruct((peers * rows, channels), shard.dtype)),
         in_specs=[pl.BlockSpec(memory_space=pltpu.VMEM)] * 2,
-        out_specs=(pl.BlockSpec(memory_space=pltpu.VMEM),) * 2,
+        out_specs=(pl.BlockSpec(memory_space=pltpu.VMEM),) * 3,
         scratch_shapes=[
             pltpu.VMEM(clips_local.shape, clips_local.dtype),
             pltpu.VMEM((cells // 64 + 2, 10, 10, channels), jnp.float32),
+            pltpu.VMEM((peers, rows, channels), shard.dtype),
+            pltpu.SemaphoreType.DMA((peers,)),
+            pltpu.SemaphoreType.DMA((peers,)),
             pltpu.SemaphoreType.DMA((micro_count,)),
             pltpu.SemaphoreType.DMA((micro_count,)),
         ],
         compiler_params=pltpu.CompilerParams(collective_id=2, has_side_effects=True),
-    )(clips_local, weight)
+    )(clips_local, shard)
 
 
 def backward_kernel(cot_ref, seen_ref, w_ref, share_ref, recv, sendbuf, pad, gpad, wg_ref, parts_ref, held, mine,
@@ -365,12 +380,12 @@
 
 def per_device(clips, cotangent, weights):
     channels = weights.shape[-1]
-    weight = gather_rows(weights[0]).reshape(-1, channels, channels)
     blocks = lax.axis_size("dp")
     micro_count = clips.shape[0]
     clips_local = clips[:, 0].reshape(micro_count, -1, channels)
     cot_local = cotangent[:, 0].reshape(micro_count, -1, channels)
-    seen, produced = forward_line(clips_local, weight)
+    seen, produced, weight = forward_line(clips_local, weights[0])
+    weight = weight.reshape(-1, channels, channels)
     grad_share = backward_line(cot_local, seen, weight, blocks)
     return (produced.reshape(clips[:, 0].shape)[None, :, None], grad_share[None])
 

time: 105 us -> 103 us (0.981)
  Pallas kernels: 102 us -> 99.7 us
    pallas_call x2 -> x1, Pallas kernels: 31.8 us -> 30.1 us  [forward_line(): pl.pallas_call(forward_kernel, out_shape=(shape, shape, jax.ShapeDtypeStr...]
where the time goes in v13:
time: 103 us
  Pallas kernels  99.7 us (97%)
  local copies, waits for them, and re-layouts  2.3 us (2%)
    pallas_call x1, Pallas kernels, backward_line(): pl.pallas_call(backward_kernel, out_shape=jax.ShapeDtypeStruct((block_row...  69.6 us
    pallas_call x1, Pallas kernels, forward_line(): pl.pallas_call(forward_kernel, out_shape=(shape, shape, jax.ShapeDtypeStr...  30.1 us
    unnamed x4, local copies, waits for them, and re-layouts  2.3 us

profile of v13, /device:TPU:6, one launch (start us, length us, event | category | flops | bytes accessed | tf_op | source)
XLA Modules:
  0.0 102.6 jit_solution(4424569540813180500)
XLA Ops:
  0.6 30.1 %shard_map.50 = (bf16[8,256,128]{2,1,0:T(8,128)(2,1)}, bf16[8,256,128]{2,1,0:T(8,128)(2,1)}, bf16[3456,128]{1,0:T(8,128)(2,1)}) custom-call(bf16[8,256,128]{2,1,0:T(8,128)(2,1)} %bitcast.9, bf16[108,128]{1,0:T(8,128)(2,1)} %bitcast.13), custom_call_target="tpu_custom_call" | custom-call | tf_op jit(solution)/shard_map/pallas_call | solution.py:274
  30.7 0.0 copy-start
  30.7 69.6 %shard_map.51 = f32[108,128]{1,0:T(8,128)} custom-call(bf16[8,256,128]{2,1,0:T(8,128)(2,1)} %bitcast.11, bf16[8,256,128]{2,1,0:T(8,128)(2,1)} %get-tuple-element.6.seen_ref, bf16[27,128,128]{2,1,0:T(8,128)(2,1)} %bitcast.8), custom_call_target="tpu_custom_call" | custom-call | tf_op jit(solution)/shard_map/pallas_call | solution.py:356
  100.3 1.5 %copy.6 = f32[1,108,128]{2,0,1:T(1,128)} copy(f32[1,108,128]{2,1,0:T(8,128)} %bitcast.12) | data formatting | bytes 110592
  101.8 0.0 copy-done
  101.8 0.8 copy.8
Async XLA Ops:
  30.7 71.1 %copy-start = (bf16[8,256,128]{2,1,0:T(8,128)(2,1)S(1)}, bf16[8,256,128]{2,1,0:T(8,128)(2,1)}, u32[]{:S(2)}) copy-start(bf16[8,256,128]{2,1,0:T(8,128)(2,1)} %get-tuple-element.5) | copy-start | bytes 1572868

commit v14 on v13

--- a/solution.py
+++ b/solution.py
@@ -152,7 +152,7 @@
     own = gather_block(side)
     cross.wait_send()
     cross.wait_recv()
-    out_ref[...] = own + mine[...]
+    out_ref[...] = (own + mine[...]).reshape(out_ref.shape)
 
 
 def scatter_rows(parts):
@@ -355,7 +355,7 @@
     block_rows = taps * channels // blocks
     return pl.pallas_call(
         backward_kernel,
-        out_shape=jax.ShapeDtypeStruct((block_rows, channels), jnp.float32),
+        out_shape=jax.ShapeDtypeStruct((block_rows, 1, channels), jnp.float32),
         in_specs=[pl.BlockSpec(memory_space=pltpu.VMEM)] * 3,
         out_specs=pl.BlockSpec(memory_space=pltpu.VMEM),
         scratch_shapes=[
@@ -387,7 +387,7 @@
     seen, produced, weight = forward_line(clips_local, weights[0])
     weight = weight.reshape(-1, channels, channels)
     grad_share = backward_line(cot_local, seen, weight, blocks)
-    return (produced.reshape(clips[:, 0].shape)[None, :, None], grad_share[None])
+    return (produced.reshape(clips[:, 0].shape)[None, :, None], grad_share.reshape((1,) + grad_share.shape[::2]))
 
 
 def solution(mesh):

time: 103 us -> 102 us (level)
    unnamed x4 -> x6, local copies, waits for them, and re-layouts: 2.3 us -> 1.43 us
where the time goes in v14:
time: 102 us
  Pallas kernels  99.7 us (98%)
  local copies, waits for them, and re-layouts  1.43 us (1%)
    pallas_call x1, Pallas kernels, backward_line(): pl.pallas_call(backward_kernel, out_shape=jax.ShapeDtypeStruct((block_row...  69.7 us
    pallas_call x1, Pallas kernels, forward_line(): pl.pallas_call(forward_kernel, out_shape=(shape, shape, jax.ShapeDtypeStr...  30 us

profile of v14, /device:TPU:6, one launch (start us, length us, event | category | flops | bytes accessed | tf_op | source)
XLA Modules:
  0.0 101.8 jit_solution(3594509489976609156)
XLA Ops:
  0.6 30.0 %shard_map.50 = (bf16[8,256,128]{2,1,0:T(8,128)(2,1)}, bf16[8,256,128]{2,1,0:T(8,128)(2,1)}, bf16[3456,128]{1,0:T(8,128)(2,1)}) custom-call(bf16[8,256,128]{2,1,0:T(8,128)(2,1)} %bitcast.10, bf16[108,128]{1,0:T(8,128)(2,1)} %bitcast.13), custom_call_target="tpu_custom_call" | custom-call | tf_op jit(solution)/shard_map/pallas_call | solution.py:274
  30.7 0.0 copy-start
  30.7 69.7 %shard_map.51 = f32[108,1,128]{2,1,0:T(1,128)} custom-call(bf16[8,256,128]{2,1,0:T(8,128)(2,1)} %bitcast.9, bf16[8,256,128]{2,1,0:T(8,128)(2,1)} %get-tuple-element.6.seen_ref, bf16[27,128,128]{2,1,0:T(8,128)(2,1)} %bitcast.8), custom_call_target="tpu_custom_call" | custom-call | tf_op jit(solution)/shard_map/pallas_call | solution.py:356
  100.4 0.0 copy-done
  100.4 0.0 copy-start.1
  100.4 0.8 copy.8
  101.2 0.0 copy-done.1
  101.2 0.6 copy.9
Async XLA Ops:
  30.7 69.7 %copy-start = (bf16[8,256,128]{2,1,0:T(8,128)(2,1)S(1)}, bf16[8,256,128]{2,1,0:T(8,128)(2,1)}, u32[]{:S(2)}) copy-start(bf16[8,256,128]{2,1,0:T(8,128)(2,1)} %get-tuple-element.5) | copy-start | bytes 1572868
  100.4 0.8 copy-start.1

commit v15 on v14

--- a/solution.py
+++ b/solution.py
@@ -311,7 +311,7 @@
 
         upstream = recv[m]
         base = seen_ref[m].astype(jnp.float32)
-        squash_into(pad, base)
+
         @pl.when(here > 0)
         def _():
             up = upstream.astype(jnp.float32)
@@ -328,14 +328,30 @@
             sendbuf[m] = (up + field * slope).astype(sendbuf.dtype)
             line_copy(sendbuf.at[m], recv.at[m], send_sem.at[m], recv_sem.at[m], here - 1, col).start()
 
+        @pl.when(here == 0)
+        def _():
+            weight_term(m)
+
+        return carry
+
+    def weight_term(m):
+        upstream = recv[m]
+        squash_into(pad, seen_ref[m].astype(jnp.float32))
         for tap, window in tap_windows(pad, 4, False):
             wg_ref[tap * 128 : (tap + 1) * 128, :] += lax.dot_general(
                 window, upstream, (((0,), (0,)), ((), ())),
                 preferred_element_type=jnp.float32,
             )
+
+    def late_term(m, carry):
+        weight_term(m)
         return carry
 
     lax.fori_loop(0, micro_count, step, 0)
+
+    @pl.when(here > 0)
+    def _():
+        lax.fori_loop(0, micro_count, late_term, 0)
 
     block_rows = parts_ref.shape[1]
     for block in range(parts_ref.shape[0]):

time: 102 us -> 99 us (0.971)
  the two profiles are of different devices: /device:TPU:6 before, /device:TPU:1 now
where the time goes in v15:
time: 99 us; the launch traced here: 98.8 us
  Pallas kernels  96.7 us (98%)
  local copies, waits for them, and re-layouts  1.43 us (1%)
    pallas_call x1, Pallas kernels, backward_line(): pl.pallas_call(backward_kernel, out_shape=jax.ShapeDtypeStruct((block_row...  61.9 us
    pallas_call x1, Pallas kernels, forward_line(): pl.pallas_call(forward_kernel, out_shape=(shape, shape, jax.ShapeDtypeStr...  34.8 us

profile of v15, /device:TPU:1, one launch (start us, length us, event | category | flops | bytes accessed | tf_op | source)
XLA Modules:
  0.0 98.8 jit_solution(17166706318807152975)
XLA Ops:
  0.6 34.8 %shard_map.50 = (bf16[8,256,128]{2,1,0:T(8,128)(2,1)}, bf16[8,256,128]{2,1,0:T(8,128)(2,1)}, bf16[3456,128]{1,0:T(8,128)(2,1)}) custom-call(bf16[8,256,128]{2,1,0:T(8,128)(2,1)} %bitcast.10, bf16[108,128]{1,0:T(8,128)(2,1)} %bitcast.13), custom_call_target="tpu_custom_call" | custom-call | tf_op jit(solution)/shard_map/pallas_call | solution.py:274
  35.4 0.0 copy-start
  35.4 61.9 %shard_map.51 = f32[108,1,128]{2,1,0:T(1,128)} custom-call(bf16[8,256,128]{2,1,0:T(8,128)(2,1)} %bitcast.9, bf16[8,256,128]{2,1,0:T(8,128)(2,1)} %get-tuple-element.6.seen_ref, bf16[27,128,128]{2,1,0:T(8,128)(2,1)} %bitcast.8), custom_call_target="tpu_custom_call" | custom-call | tf_op jit(solution)/shard_map/pallas_call | solution.py:372
  97.4 0.0 copy-done
  97.4 0.0 copy-start.1
  97.4 0.8 copy.8
  98.2 0.0 copy-done.1
  98.2 0.6 copy.9
Async XLA Ops:
  35.4 61.9 %copy-start = (bf16[8,256,128]{2,1,0:T(8,128)(2,1)S(1)}, bf16[8,256,128]{2,1,0:T(8,128)(2,1)}, u32[]{:S(2)}) copy-start(bf16[8,256,128]{2,1,0:T(8,128)(2,1)} %get-tuple-element.5) | copy-start | bytes 1572868
  97.4 0.8 copy-start.1

commit v16 on v15

--- a/solution.py
+++ b/solution.py
@@ -289,7 +289,7 @@
     )(clips_local, shard)
 
 
-def backward_kernel(cot_ref, seen_ref, w_ref, share_ref, recv, sendbuf, pad, gpad, wg_ref, parts_ref, held, mine,
+def backward_kernel(cot_ref, seen_ref, w_ref, share_ref, recv, sendbuf, pad, gpad, wg_ref, wg_t, parts_ref, held, mine,
                     theirs, send_sem, recv_sem, share_send, share_recv, cross_sem):
     count = lax.axis_size("section")
     here = lax.axis_index("section")
@@ -298,7 +298,7 @@
     greet_group(col, here, greet_line(here, count, col, settle=False))
     pad[...] = jnp.zeros_like(pad)
     gpad[...] = jnp.zeros_like(gpad)
-    wg_ref[...] = jnp.zeros_like(wg_ref)
+    wg_t[...] = jnp.zeros_like(wg_t)
 
     def step(m, carry):
         @pl.when(here == count - 1)
@@ -335,13 +335,10 @@
         return carry
 
     def weight_term(m):
-        upstream = recv[m]
+        upstream_t = recv[m].T
         squash_into(pad, seen_ref[m].astype(jnp.float32))
         for tap, window in tap_windows(pad, 4, False):
-            wg_ref[tap * 128 : (tap + 1) * 128, :] += lax.dot_general(
-                window, upstream, (((0,), (0,)), ((), ())),
-                preferred_element_type=jnp.float32,
-            )
+            wg_t[:, tap * 128 : (tap + 1) * 128] += jnp.dot(upstream_t, window, preferred_element_type=jnp.float32)
 
     def late_term(m, carry):
         weight_term(m)
@@ -353,6 +350,8 @@
     def _():
         lax.fori_loop(0, micro_count, late_term, 0)
 
+    for tap in range(wg_ref.shape[0] // 128):
+        wg_ref[tap * 128 : (tap + 1) * 128, :] = wg_t[:, tap * 128 : (tap + 1) * 128].T
     block_rows = parts_ref.shape[1]
     for block in range(parts_ref.shape[0]):
         parts_ref[block] = wg_ref[block * block_rows : (block + 1) * block_rows, :].astype(parts_ref.dtype)
@@ -380,6 +379,7 @@
             pltpu.VMEM((cells // 64 + 2, 10, 10, channels), jnp.float32),
             pltpu.VMEM((cells // 64 + 4, 10, 10, channels), jnp.float32),
             pltpu.VMEM((taps * channels, channels), jnp.float32),
+            pltpu.VMEM((channels, taps * channels), jnp.float32),
             pltpu.VMEM((blocks, block_rows, channels), jnp.bfloat16),
             pltpu.VMEM((blocks // 2, 2, block_rows, channels), jnp.bfloat16),
             pltpu.VMEM((block_rows, channels), jnp.float32),

time: 99 us -> 99.5 us (level)
  no operation moved by 1% of the time
where the time goes in v16:
time: 99.5 us; the launch traced here: 99.4 us
  Pallas kernels  97.3 us (98%)
  local copies, waits for them, and re-layouts  1.43 us (1%)
    pallas_call x1, Pallas kernels, backward_line(): pl.pallas_call(backward_kernel, out_shape=jax.ShapeDtypeStruct((block_row...  62.5 us
    pallas_call x1, Pallas kernels, forward_line(): pl.pallas_call(forward_kernel, out_shape=(shape, shape, jax.ShapeDtypeStr...  34.8 us

profile of v16, /device:TPU:1, one launch (start us, length us, event | category | flops | bytes accessed | tf_op | source)
XLA Modules:
  0.0 99.4 jit_solution(2860693007621826351)
XLA Ops:
  0.6 34.8 %shard_map.50 = (bf16[8,256,128]{2,1,0:T(8,128)(2,1)}, bf16[8,256,128]{2,1,0:T(8,128)(2,1)}, bf16[3456,128]{1,0:T(8,128)(2,1)}) custom-call(bf16[8,256,128]{2,1,0:T(8,128)(2,1)} %bitcast.10, bf16[108,128]{1,0:T(8,128)(2,1)} %bitcast.13), custom_call_target="tpu_custom_call" | custom-call | tf_op jit(solution)/shard_map/pallas_call | solution.py:274
  35.4 0.0 copy-start
  35.4 62.5 %shard_map.51 = f32[108,1,128]{2,1,0:T(1,128)} custom-call(bf16[8,256,128]{2,1,0:T(8,128)(2,1)} %bitcast.9, bf16[8,256,128]{2,1,0:T(8,128)(2,1)} %get-tuple-element.6.seen_ref, bf16[27,128,128]{2,1,0:T(8,128)(2,1)} %bitcast.8), custom_call_target="tpu_custom_call" | custom-call | tf_op jit(solution)/shard_map/pallas_call | solution.py:371
  97.9 0.0 copy-done
  97.9 0.0 copy-start.1
  97.9 0.8 copy.8
  98.7 0.0 copy-done.1
  98.7 0.6 copy.9
Async XLA Ops:
  35.4 62.5 %copy-start = (bf16[8,256,128]{2,1,0:T(8,128)(2,1)S(1)}, bf16[8,256,128]{2,1,0:T(8,128)(2,1)}, u32[]{:S(2)}) copy-start(bf16[8,256,128]{2,1,0:T(8,128)(2,1)} %get-tuple-element.5) | copy-start | bytes 1572868
  97.9 0.8 copy-start.1

commit v17 on v15

--- a/solution.py
+++ b/solution.py
@@ -146,13 +146,13 @@
 
         return lax.fori_loop(1, planes, finish, parts_ref[2 * slot + block].astype(jnp.float32))
 
-    theirs[...] = gather_block(far)
+    theirs[...] = gather_block(far).astype(theirs.dtype)
     cross = group_copy(theirs, mine, cross_sem.at[0], cross_sem.at[1], row, partner)
     cross.start()
     own = gather_block(side)
     cross.wait_send()
     cross.wait_recv()
-    out_ref[...] = (own + mine[...]).reshape(out_ref.shape)
+    out_ref[...] = (own + mine[...].astype(jnp.float32)).reshape(out_ref.shape)
 
 
 def scatter_rows(parts):
@@ -382,8 +382,8 @@
             pltpu.VMEM((taps * channels, channels), jnp.float32),
             pltpu.VMEM((blocks, block_rows, channels), jnp.bfloat16),
             pltpu.VMEM((blocks // 2, 2, block_rows, channels), jnp.bfloat16),
-            pltpu.VMEM((block_rows, channels), jnp.float32),
-            pltpu.VMEM((block_rows, channels), jnp.float32),
+            pltpu.VMEM((block_rows, channels), jnp.bfloat16),
+            pltpu.VMEM((block_rows, channels), jnp.bfloat16),
             pltpu.SemaphoreType.DMA((micro_count,)),
             pltpu.SemaphoreType.DMA((micro_count,)),
             pltpu.SemaphoreType.DMA((blocks // 2, 2)),

time: 99 us -> 98.4 us (level)
  no operation moved by 1% of the time
where the time goes in v17:
time: 98.4 us; the launch traced here: 98.2 us
  Pallas kernels  96.1 us (98%)
  local copies, waits for them, and re-layouts  1.43 us (1%)
    pallas_call x1, Pallas kernels, backward_line(): pl.pallas_call(backward_kernel, out_shape=jax.ShapeDtypeStruct((block_row...  61.4 us
    pallas_call x1, Pallas kernels, forward_line(): pl.pallas_call(forward_kernel, out_shape=(shape, shape, jax.ShapeDtypeStr...  34.8 us

profile of v17, /device:TPU:1, one launch (start us, length us, event | category | flops | bytes accessed | tf_op | source)
XLA Modules:
  0.0 98.2 jit_solution(9272429099801451927)
XLA Ops:
  0.6 34.8 %shard_map.50 = (bf16[8,256,128]{2,1,0:T(8,128)(2,1)}, bf16[8,256,128]{2,1,0:T(8,128)(2,1)}, bf16[3456,128]{1,0:T(8,128)(2,1)}) custom-call(bf16[8,256,128]{2,1,0:T(8,128)(2,1)} %bitcast.10, bf16[108,128]{1,0:T(8,128)(2,1)} %bitcast.13), custom_call_target="tpu_custom_call" | custom-call | tf_op jit(solution)/shard_map/pallas_call | solution.py:274
  35.4 0.0 copy-start
  35.4 61.4 %shard_map.51 = f32[108,1,128]{2,1,0:T(1,128)} custom-call(bf16[8,256,128]{2,1,0:T(8,128)(2,1)} %bitcast.9, bf16[8,256,128]{2,1,0:T(8,128)(2,1)} %get-tuple-element.6.seen_ref, bf16[27,128,128]{2,1,0:T(8,128)(2,1)} %bitcast.8), custom_call_target="tpu_custom_call" | custom-call | tf_op jit(solution)/shard_map/pallas_call | solution.py:372
  96.8 0.0 copy-done
  96.8 0.0 copy-start.1
  96.8 0.8 copy.8
  97.6 0.0 copy-done.1
  97.6 0.6 copy.9
Async XLA Ops:
  35.4 61.4 %copy-start = (bf16[8,256,128]{2,1,0:T(8,128)(2,1)S(1)}, bf16[8,256,128]{2,1,0:T(8,128)(2,1)}, u32[]{:S(2)}) copy-start(bf16[8,256,128]{2,1,0:T(8,128)(2,1)} %get-tuple-element.5) | copy-start | bytes 1572868
  96.8 0.8 copy-start.1
